TPU v7x, 512 devices: a whole 4x8x8 slice. The times are simulated.
512 devices in a mesh: leaf: 128 (over z, y, core), rhs: 4 (over x).
Axes of the slice: x: 4, y: 8, z: 8, core: 2. Of those that a mesh axis runs over, the one named last changes fastest.
Arguments:
- leaf_rhs: float32 [2, 64, 65536], P(None, 'rhs', 'leaf'), may hold values from -6 to 6
- sep_rhs: float32 [2, 64, 7, 1024], P(None, 'rhs', None, 'leaf'), may hold values from -6 to 6
- leaf_inv: bfloat16 [2, 512, 65536], P(None, 'rhs', 'leaf'), may hold values from -0.1875 to 0.1875
- leaf_low: bfloat16 [2, 512, 1024], P(None, None, 'leaf'), may hold values from -0.1875 to 0.1875
- sep_inv: bfloat16 [2, 8, 260096], P(None, None, 'leaf'), as said below
- sep_low: bfloat16 [2, 8, 129024], P(None, None, 'leaf'), as said below
- leaf_live: int32 [128], P('leaf'), may hold values from 1 to 4
- targets: int32 [7, 128], replicated, may hold values from 0 to 127, as said below
Outputs:
- leaf_solution: float32 [2, 64, 65536], P(None, 'rhs', 'leaf')
- sep_solution: float32 [2, 64, 7, 1024], P(None, 'rhs', None, 'leaf')
Inputs may be any that keep to these rules, and one draw needn't show every extreme that they name: `targets`: in row l, the entries of each aligned group of 2 ** (l + 1) devices are a permutation of 0 to 2 ** (l + 1) - 1. Rows of a leaf front beyond 128 * leaf_live are padding and are ignored. `sep_inv`: entries are independent, of mean zero, with spread inversely proportional to the square root of the front's order. `sep_low`: entries are independent, of mean zero, with spread inversely proportional to the square root of the front's order.
All inputs are finite; a program needn't handle non-finite values.
Results may differ from a plain program's by a relative error of at most 0.025.
Values may be sent and summed in bfloat16 or wider, within the bound.
A program may use at most 64 MiB of HBM per device.

v0:
```python
import jax
import jax.numpy as jnp
from jax import lax
from jax.experimental import pallas as pl
from jax.experimental.pallas import tpu as pltpu
from jax.sharding import PartitionSpec as P

MESH = pl.DeviceIdType.MESH
bf16 = jnp.bfloat16
f32 = jnp.float32

COUNTS = dict(
    msg=15, zx=3, c0=7, c1=7, c2=7, c3=7, c4=7, t0=1, t1=1, t2=1, t3=1, t4=1,
    u4=1, u5=3, u6=7, w7=7, x7=7, x6=3, x5=1, w5=1, w6=3, lw=3,
)
FIRST = {}
_total = 0
for _name, _count in COUNTS.items():
    FIRST[_name] = _total
    _total += _count
COPIES = _total


def mm(a, b):
    return jnp.dot(a, b, preferred_element_type=f32)


def mm_nt(a, b):
    return lax.dot_general(a, b, (((1,), (1,)), ((), ())), preferred_element_type=f32)


def flip(value, mask):
    out = value
    for bit in range(3):
        if mask >> bit & 1:
            here = lax.rem(lax.div(value, 1 << bit), 2)
            out = out + (1 - 2 * here) * (1 << bit)
    return out


def iota(shape, axis):
    return lax.broadcasted_iota(jnp.int32, shape, axis)


def kernel(
    rhs_ref, sep_ref, inv_ref, low_ref, sinv_ref, slow_ref, live_ref, tgt_ref,
    leaf_out, sep_out,
    st, pk, m0, c0, c1, c2, c3, c4, zxs, zxr, eh, tt, p0, pis, pi4, rs_, vs, bs,
    m123, m4, m5, m6, i14, i5, i6, i7,
    s4, r4, s5, r5, s6, r6, s7, r7, xb7, xb6, xb5, sw5, rw5, sw6, rw6, w5o, w6o,
    lws, lwr, lwo, xo, xt, ssem, rsem,
):
    leaf = lax.axis_index("leaf")
    x = lax.axis_index("rhs")
    c = lax.rem(leaf, 2)
    y = lax.rem(lax.div(leaf, 2), 8)
    z = lax.div(leaf, 16)
    dl = lax.rem(leaf, 16)

    def dev(zz, yy, cc, xx):
        return (zz * 16 + yy * 2 + cc, xx)

    layer = [(k >> 1, k & 1) for k in range(1, 16)]
    barrier = pltpu.get_barrier_semaphore()

    def greet(device):
        pl.semaphore_signal(barrier, inc=1, device_id=device, device_id_type=MESH)

    for ky, kc in layer:
        greet(dev(z, flip(y, ky), flip(c, kc), x))
    for k in range(1, 8):
        greet(dev(flip(z, k), y, c, x))
    for k in range(1, 4):
        greet(dev(z, y, c, flip(x, k)))

    pending = []

    def copy(name, j, src, dst, device):
        index = FIRST[name] + j
        return pltpu.make_async_remote_copy(
            src_ref=src, dst_ref=dst, send_sem=ssem.at[index], recv_sem=rsem.at[index],
            device_id=device, device_id_type=MESH,
        )

    def send(name, j, src, dst, device):
        out = copy(name, j, src, dst, device)
        out.start()
        pending.append(out)
        return out

    live = live_ref[0]
    mask = iota((1, 512), 1) < live * 128
    zr = jnp.where(mask, rhs_ref[0], 0.0).astype(bf16)
    zi = jnp.where(mask, rhs_ref[1], 0.0).astype(bf16)
    er = low_ref[0].astype(f32)
    ei = low_ref[1].astype(f32)
    ehv = jnp.concatenate(
        [jnp.concatenate([er, -ei], axis=1), jnp.concatenate([ei, er], axis=1)], axis=0
    ).astype(bf16)
    eh[...] = ehv
    zcat = jnp.concatenate([zr, zi], axis=1)
    st[:, 112:128] = mm_nt(ehv, zcat)
    for level in range(7):
        st[0:8, 16 * level : 16 * level + 16] = sep_ref[0, level]
        st[8:16, 16 * level : 16 * level + 16] = sep_ref[1, level]
    m0[y, c] = st[...].astype(bf16)
    for q in range(4):
        zxs[q, 0] = zr[:, 128 * q : 128 * q + 128]
        zxs[q, 1] = zi[:, 128 * q : 128 * q + 128]
    zxr[x] = zxs[x]
    pk[:, 0:128] = jnp.zeros((16, 128), f32)
    pk[:, 1024:1152] = jnp.zeros((16, 128), f32)
    for part in range(2):
        pk[8 * part : 8 * part + 8, 16:1024] = slow_ref[part].astype(f32)
        pk[8 * part : 8 * part + 8, 1040:3072] = sinv_ref[part].astype(f32)
    c0[y, c, :, 0:256] = pk[:, 0:256].astype(bf16)
    c0[y, c, :, 256:512] = pk[:, 1024:1280].astype(bf16)
    c1[y, c] = pk[:, 256:512].astype(bf16)
    c2[y, c] = pk[:, 512:1024].astype(bf16)
    c3[y, c] = pk[:, 2048:3072].astype(bf16)
    c4[y, c] = pk[:, 1280:2048].astype(bf16)

    pl.semaphore_wait(barrier, 25)

    got = {name: [] for name in COUNTS}
    for j, (ky, kc) in enumerate(layer):
        got["msg"].append(
            send("msg", j, m0.at[y, c], m0.at[y, c], dev(z, flip(y, ky), flip(c, kc), x))
        )
    chunks = [("c0", c0), ("c1", c1), ("c2", c2), ("c3", c3), ("c4", c4)]

    def scatter(name, buf):
        for k in range(1, 8):
            got[name].append(
                send(name, k - 1, buf.at[y, c], buf.at[y, c], dev(z, flip(y, k), c, x))
            )

    scatter("c0", c0)
    for k in range(1, 4):
        got["zx"].append(
            send("zx", k - 1, zxs.at[flip(x, k)], zxr.at[x], dev(z, y, c, flip(x, k)))
        )
    for name, buf in chunks[1:]:
        scatter(name, buf)

    def arrive(name):
        for one in got[name]:
            one.wait_recv()

    def twin(index):
        name, buf = chunks[index]
        arrive(name)
        got["t%d" % index].append(
            send("t%d" % index, 0, buf.at[:, c], buf.at[:, c], dev(z, y, 1 - c, x))
        )

    tgt = tgt_ref[...].astype(f32).astype(bf16)
    row = iota((256, 128), 0)
    col = iota((256, 128), 1)
    quad = lax.div(z, 4) * 4
    for s in range(4):
        pick = col == (quad + s) * 16 + (row % 128) // 8
        tt[s] = mm_nt(pick.astype(f32).astype(bf16), tgt)
    pick = col == z * 16 + row // 16
    own0 = mm_nt(pick.astype(f32).astype(bf16), tgt)
    lane = iota((256, 256), 1).astype(f32)
    rown = iota((256, 1), 0)
    inner = (rown // 128 * 8 + rown % 8).astype(f32)
    p0[...] = (
        lane == (rown // 32 * 32 + rown % 16).astype(f32) + 16.0 * own0[:, 0:1]
    ).astype(f32).astype(bf16)
    zq = lax.rem(z, 4)
    zp = lax.rem(z, 2)
    mine = tt[zq]
    for level in range(1, 4):
        base = (rown % 128 // 8 // (2 << level) * (2 << level) * 16).astype(f32) + inner
        pis[level - 1] = (lane == base + 16.0 * mine[:, level : level + 1]).astype(f32).astype(bf16)
    for t in range(2):
        pi4[t] = (
            lane + 256.0 * t == inner + 16.0 * mine[:, 4:5]
        ).astype(f32).astype(bf16)
    natural = (lane == (rown % 128 // 8 * 16).astype(f32) + inner).astype(f32).astype(bf16)
    sign_row = (1 - 2 * (iota((256, 1), 0) // 8 % 2)).astype(f32)
    sign_lane = (1 - 2 * (iota((1, 256), 1) // 8 % 2)).astype(f32)

    def embed(raw):
        parts = raw.reshape(16, 2, 8, 128)
        swapped = jnp.concatenate([parts[:, 1:2], parts[:, 0:1]], axis=1).reshape(256, 128)
        return jnp.concatenate([raw * sign_row, swapped], axis=1).astype(bf16)

    def small(raw, level):
        size = 8 << level
        at = iota((128, 128), 0)
        to = iota((128, 128), 1)
        repeat = (at == size + to % size).astype(f32).astype(bf16)
        wide = mm(raw, repeat)
        front = iota((256, 128), 0) // (16 << level) == iota((256, 128), 1) // size
        return embed(jnp.where(front, wide, 0.0))

    arrive("msg")
    flipped = jnp.transpose(m0[...].reshape(256, 128).astype(f32))
    rs_[...] = flipped
    u = mm(flipped[112:128].astype(bf16), p0[...])
    twin(0)
    v = (flipped[0:16] - u).astype(bf16)
    vs[0] = v
    arrive("t0")
    raw0 = c0[:, :, :, 0:128].reshape(256, 128)
    for level in range(1, 4):
        m123[level - 1] = mm(small(raw0, level), pis[level - 1]).astype(bf16)
        u = mm(v, m123[level - 1])
        v = (rs_[16 * level : 16 * level + 16] - u).astype(bf16)
        vs[level] = v
    b4 = embed(c0[:, :, :, 128:256].reshape(256, 128).astype(f32))
    for t in range(2):
        m4[t] = mm(b4, pi4[t]).astype(bf16)
    s4[...] = mm(v, m4[1 - zp]).astype(bf16)
    got["u4"].append(send("u4", 0, s4, r4, dev(flip(z, 1), y, c, x)))
    u = mm(v, m4[zp])

    twin(1)
    arrive("t1")
    pair = lax.div(zq, 2) * 2
    for s in range(2):
        bs[s] = embed(c1[:, :, :, 128 * s : 128 * s + 128].reshape(256, 128).astype(f32))

    def fold5(t, carry):
        shift = (256 * t).astype(f32)
        total = jnp.zeros((256, 256), f32)
        for s in range(2):
            hot = lane + shift == inner + 16.0 * tt[pair + s][:, 5:6]
            total = total + mm(bs[s], hot.astype(f32).astype(bf16))
        m5[t] = total.astype(bf16)
        return carry

    lax.fori_loop(0, 4, fold5, 0)
    arrive("u4")
    v = (rs_[64:80] - u - r4[...].astype(f32)).astype(bf16)
    vs[4] = v
    for k in range(1, 4):
        s5[k - 1] = mm(v, m5[flip(zq, k)]).astype(bf16)
        got["u5"].append(send("u5", k - 1, s5.at[k - 1], r5.at[k - 1], dev(flip(z, k), y, c, x)))
    u = mm(v, m5[zq])

    twin(2)
    arrive("t2")
    for s in range(4):
        bs[s] = embed(c2[:, :, :, 128 * s : 128 * s + 128].reshape(256, 128).astype(f32))

    def fold6(t, carry):
        shift = (256 * t).astype(f32)
        total = jnp.zeros((256, 256), f32)
        for s in range(4):
            hot = lane + shift == inner + 16.0 * tt[s][:, 6:7]
            total = total + mm(bs[s], hot.astype(f32).astype(bf16))
        m6[t] = total.astype(bf16)
        return carry

    lax.fori_loop(0, 8, fold6, 0)
    arrive("u5")
    v = rs_[80:96] - u
    for k in range(3):
        v = v - r5[k].astype(f32)
    v = v.astype(bf16)
    vs[5] = v
    for k in range(1, 8):
        s6[k - 1] = mm(v, m6[flip(z, k)]).astype(bf16)
        got["u6"].append(send("u6", k - 1, s6.at[k - 1], r6.at[k - 1], dev(flip(z, k), y, c, x)))
    u = mm(v, m6[z])

    twin(3)
    arrive("t3")
    for s in range(8):
        i7[s] = mm(
            embed(c3[:, :, :, 128 * s : 128 * s + 128].reshape(256, 128).astype(f32)), natural
        ).astype(bf16)
    arrive("u6")
    v = rs_[96:112] - u
    for k in range(7):
        v = v - r6[k].astype(f32)
    v = v.astype(bf16)
    for k in range(1, 8):
        s7[k - 1] = mm(v, i7[flip(z, k)]).astype(bf16)
        got["w7"].append(send("w7", k - 1, s7.at[k - 1], r7.at[k - 1], dev(flip(z, k), y, c, x)))
    top = mm(v, i7[z])

    twin(4)
    arrive("t4")
    for s in range(2):
        i5[s] = mm(
            embed(c4[:, :, :, 128 * s : 128 * s + 128].reshape(256, 128).astype(f32)), natural
        ).astype(bf16)
    for s in range(4):
        i6[s] = mm(
            embed(c4[:, :, :, 256 + 128 * s : 384 + 128 * s].reshape(256, 128).astype(f32)), natural
        ).astype(bf16)
    sw5[...] = mm(vs[4], i5[1 - zp]).astype(bf16)
    got["w5"].append(send("w5", 0, sw5, rw5, dev(flip(z, 1), y, c, x)))
    for k in range(1, 4):
        sw6[k - 1] = mm(vs[5], i6[flip(zq, k)]).astype(bf16)
        got["w6"].append(send("w6", k - 1, sw6.at[k - 1], rw6.at[k - 1], dev(flip(z, k), y, c, x)))
    w5o[...] = mm(vs[4], i5[zp])
    w6o[...] = mm(vs[5], i6[zq])

    arrive("w7")
    for k in range(7):
        top = top + r7[k].astype(f32)
    top = top * sign_lane
    xo[96:112] = top
    xb7[z] = top.astype(bf16)
    for k in range(1, 8):
        got["x7"].append(send("x7", k - 1, xb7.at[z], xb7.at[z], dev(flip(z, k), y, c, x)))

    arrive("zx")
    zr4 = zxr[:, 0].reshape(64, 128)
    zi4 = zxr[:, 1].reshape(64, 128)
    panel = inv_ref[...].reshape(256, 512)
    real = mm(jnp.concatenate([zr4, -zi4], axis=1), panel).reshape(4, 16, 512)
    imag = mm(jnp.concatenate([zi4, zr4], axis=1), panel).reshape(4, 16, 512)
    lwo[:, 0] = real
    lwo[:, 1] = imag
    lws[:, 0] = real.astype(bf16)
    lws[:, 1] = imag.astype(bf16)
    for k in range(1, 4):
        got["lw"].append(
            send("lw", k - 1, lws.at[flip(x, k)], lwr.at[k - 1], dev(z, y, c, flip(x, k)))
        )

    rawi = c0[:, :, :, 256:384].reshape(256, 128)
    for level in range(1, 4):
        i14[level - 1] = mm(small(rawi, level), natural).astype(bf16)
    i14[3] = mm(embed(c0[:, :, :, 384:512].reshape(256, 128).astype(f32)), natural).astype(bf16)
    for level in range(1, 5):
        xo[16 * level - 16 : 16 * level] = mm(vs[level - 1], i14[level - 1]) * sign_lane
    arrive("w5")
    arrive("w6")
    xo[64:80] = (w5o[...] + rw5[...].astype(f32)) * sign_lane
    w6 = w6o[...]
    for k in range(3):
        w6 = w6 + rw6[k].astype(f32)
    w6 = w6 * sign_lane

    arrive("x7")
    for t in range(8):
        w6 = w6 - mm_nt(xb7[t], m6[t])
    xo[80:96] = w6
    xb6[zq] = w6.astype(bf16)
    for k in range(1, 4):
        got["x6"].append(send("x6", k - 1, xb6.at[zq], xb6.at[zq], dev(flip(z, k), y, c, x)))
    arrive("x6")
    w5 = xo[64:80]
    for t in range(4):
        w5 = w5 - mm_nt(xb6[t], m5[t])
    xo[64:80] = w5
    xb5[zp] = w5.astype(bf16)
    got["x5"].append(send("x5", 0, xb5.at[zp], xb5.at[zp], dev(flip(z, 1), y, c, x)))
    arrive("x5")
    now = xo[48:64]
    for t in range(2):
        now = now - mm_nt(xb5[t], m4[t])
    xo[48:64] = now
    for level in range(3, 0, -1):
        now = xo[16 * level - 16 : 16 * level] - mm_nt(now.astype(bf16), m123[level - 1])
        xo[16 * level - 16 : 16 * level] = now
    start = pl.multiple_of(dl * 16, 16)
    back = mm_nt(now.astype(bf16), p0[pl.ds(start, 16), :]).astype(bf16)
    less = mm(back, eh[...])
    arrive("lw")
    own = lwo[x]
    for k in range(3):
        own = own + lwr[k].astype(f32)
    leaf_out[0] = jnp.where(mask, own[0] - less[:, 0:512], 0.0)
    leaf_out[1] = jnp.where(mask, own[1] + less[:, 512:1024], 0.0)
    xo[112:128] = jnp.zeros((16, 256), f32)
    xt[...] = jnp.transpose(xo[...])
    mineT = xt[pl.ds(start, 16), :]
    for level in range(7):
        sep_out[0, level] = mineT[0:8, 16 * level : 16 * level + 16]
        sep_out[1, level] = -mineT[8:16, 16 * level : 16 * level + 16]

    for one in pending:
        one.wait_send()


def body(leaf_rhs, sep_rhs, leaf_inv, leaf_low, sep_inv, sep_low, leaf_live, targets):
    vm = pl.BlockSpec(memory_space=pltpu.VMEM)
    sm = pl.BlockSpec(memory_space=pltpu.SMEM)
    V = pltpu.VMEM
    out_leaf, out_sep = pl.pallas_call(
        kernel,
        out_shape=(
            jax.ShapeDtypeStruct((2, 16, 512), f32),
            jax.ShapeDtypeStruct((2, 7, 8, 16), f32),
        ),
        in_specs=[vm, vm, vm, vm, vm, vm, sm, vm],
        out_specs=(vm, vm),
        scratch_shapes=[
            V((16, 128), f32), V((16, 3072), f32), V((8, 2, 16, 128), bf16),
            V((8, 2, 16, 512), bf16), V((8, 2, 16, 256), bf16), V((8, 2, 16, 512), bf16),
            V((8, 2, 16, 1024), bf16), V((8, 2, 16, 768), bf16),
            V((4, 2, 16, 128), bf16), V((4, 2, 16, 128), bf16), V((16, 1024), bf16),
            V((4, 256, 7), f32), V((256, 256), bf16), V((3, 256, 256), bf16),
            V((2, 256, 256), bf16), V((128, 256), f32), V((6, 16, 256), bf16),
            V((4, 256, 256), bf16),
            V((3, 256, 256), bf16), V((2, 256, 256), bf16), V((4, 256, 256), bf16),
            V((8, 256, 256), bf16), V((4, 256, 256), bf16), V((2, 256, 256), bf16),
            V((4, 256, 256), bf16), V((8, 256, 256), bf16),
            V((16, 256), bf16), V((16, 256), bf16), V((3, 16, 256), bf16), V((3, 16, 256), bf16),
            V((7, 16, 256), bf16), V((7, 16, 256), bf16), V((7, 16, 256), bf16),
            V((7, 16, 256), bf16), V((8, 16, 256), bf16), V((4, 16, 256), bf16),
            V((2, 16, 256), bf16), V((16, 256), bf16), V((16, 256), bf16),
            V((3, 16, 256), bf16), V((3, 16, 256), bf16), V((16, 256), f32), V((16, 256), f32),
            V((4, 2, 16, 512), bf16), V((3, 2, 16, 512), bf16), V((4, 2, 16, 512), f32),
            V((128, 256), f32), V((256, 128), f32),
            pltpu.SemaphoreType.DMA((COPIES,)), pltpu.SemaphoreType.DMA((COPIES,)),
        ],
        compiler_params=pltpu.CompilerParams(
            collective_id=0, has_side_effects=True, vmem_limit_bytes=40 * 2**20
        ),
    )(
        leaf_rhs, sep_rhs.transpose(0, 2, 3, 1), leaf_inv, leaf_low.transpose(0, 2, 1),
        sep_inv, sep_low, leaf_live, targets,
    )
    return out_leaf, out_sep.transpose(0, 3, 1, 2)


def solution(mesh):
    placed = (
        P(None, "rhs", "leaf"),
        P(None, "rhs", None, "leaf"),
        P(None, "rhs", "leaf"),
        P(None, None, "leaf"),
        P(None, None, "leaf"),
        P(None, None, "leaf"),
        P("leaf"),
        P(),
    )
    return jax.shard_map(
        body,
        mesh=mesh,
        in_specs=placed,
        out_specs=(P(None, "rhs", "leaf"), P(None, "rhs", None, "leaf")),
        check_vma=False,
    )
```

profile of v0, /device:TPU:2, one launch (start us, length us, event | category | flops | bytes accessed | tf_op | source)
XLA Modules:
  0.0 65.2 jit_solution(7346031004601344964)
XLA Ops:
  0.6 0.0 copy-start.6
  1.3 0.0 copy-done.6
  1.3 0.0 copy-start
  1.3 0.9 %copy-done = bf16[2,128,512]{2,1,0:T(8,128)(2,1)S(1)} copy-done((bf16[2,128,512]{2,1,0:T(8,128)(2,1)S(1)}, bf16[2,128,512]{2,1,0:T(8,128)(2,1)}, u32[]{:S(2)}) %copy-start) | copy-done | bytes 262168
  2.3 0.0 copy-start.1
  2.3 0.8 %copy-done.1 = f32[2,16,512]{2,1,0:T(8,128)S(1)} copy-done((f32[2,16,512]{2,1,0:T(8,128)S(1)}, f32[2,16,512]{2,1,0:T(8,128)}, u32[]{:S(2)}) %copy-start.1) | copy-done | bytes 65560
  3.1 0.0 copy-start.2
  3.1 0.8 %copy-done.2 = bf16[2,8,2032]{2,1,0:T(8,128)(2,1)S(1)} copy-done((bf16[2,8,2032]{2,1,0:T(8,128)(2,1)S(1)}, bf16[2,8,2032]{2,1,0:T(8,128)(2,1)}, u32[]{:S(2)}) %copy-start.2) | copy-done | bytes 65048
  4.0 0.0 copy-start.3
  4.0 0.8 %copy-done.3 = f32[2,16,7,8]{1,3,2,0:T(8,128)S(1)} copy-done((f32[2,16,7,8]{1,3,2,0:T(8,128)S(1)}, f32[2,16,7,8]{1,3,2,0:T(8,128)}, u32[]{:S(2)}) %copy-start.3) | copy-done | bytes 7192
  4.8 0.0 copy-start.4
  4.8 0.8 %copy-done.4 = bf16[2,8,1008]{2,1,0:T(8,128)(2,1)S(1)} copy-done((bf16[2,8,1008]{2,1,0:T(8,128)(2,1)S(1)}, bf16[2,8,1008]{2,1,0:T(8,128)(2,1)}, u32[]{:S(2)}) %copy-start.4) | copy-done | bytes 32280
  5.5 0.0 copy-start.5
  5.5 0.7 %copy-done.5 = bf16[2,512,8]{1,2,0:T(8,128)(2,1)S(1)} copy-done((bf16[2,512,8]{1,2,0:T(8,128)(2,1)S(1)}, bf16[2,512,8]{1,2,0:T(8,128)(2,1)}, u32[]{:S(2)}) %copy-start.5) | copy-done | bytes 16408
  6.2 57.7 %shard_map.95 = (f32[2,16,512]{2,1,0:T(8,128)S(1)}, f32[2,7,8,16]{3,2,1,0:T(8,128)S(1)}) custom-call(f32[2,16,512]{2,1,0:T(8,128)S(1)} %copy-done.1, f32[2,7,8,16]{3,2,1,0:T(8,128)S(1)} %bitcast.3, bf16[2,128,512]{2,1,0:T(8,128)(2,1)S(1)} %copy-done, bf16[2,8,512]{2,1,0:T(8,128)(2,1)S(1)} %bitcast.5, bf16[2,8,2032]{2,1,0:T(8,128)(2,1)S(1)} %copy-done.2, ...), custom_call_target="tpu_custom_call" | custom-call | tf_op jit(solution)/shard_map/pallas_call | solution.py:389
  63.9 0.6 copy.13
  64.6 0.6 copy.14
Async XLA Ops:
  0.6 0.7 %copy-start.6 = (s32[7,128]{1,0:T(8,128)S(1)}, s32[7,128]{1,0:T(8,128)}, u32[]{:S(2)}) copy-start(s32[7,128]{1,0:T(8,128)} %tgt_ref.1) | copy-start | bytes 10756
  1.3 0.9 %copy-start = (bf16[2,128,512]{2,1,0:T(8,128)(2,1)S(1)}, bf16[2,128,512]{2,1,0:T(8,128)(2,1)}, u32[]{:S(2)}) copy-start(bf16[2,128,512]{2,1,0:T(8,128)(2,1)} %inv_ref.1) | copy-start | bytes 786436
  2.3 0.8 %copy-start.1 = (f32[2,16,512]{2,1,0:T(8,128)S(1)}, f32[2,16,512]{2,1,0:T(8,128)}, u32[]{:S(2)}) copy-start(f32[2,16,512]{2,1,0:T(8,128)} %rhs_ref.1) | copy-start | bytes 196612
  3.1 0.8 %copy-start.2 = (bf16[2,8,2032]{2,1,0:T(8,128)(2,1)S(1)}, bf16[2,8,2032]{2,1,0:T(8,128)(2,1)}, u32[]{:S(2)}) copy-start(bf16[2,8,2032]{2,1,0:T(8,128)(2,1)} %sinv_ref.1) | copy-start | bytes 195076
  4.0 0.8 %copy-start.3 = (f32[2,16,7,8]{1,3,2,0:T(8,128)S(1)}, f32[2,16,7,8]{1,3,2,0:T(8,128)}, u32[]{:S(2)}) copy-start(f32[2,16,7,8]{1,3,2,0:T(8,128)} %param.9) | copy-start | bytes 21508
  4.8 0.8 %copy-start.4 = (bf16[2,8,1008]{2,1,0:T(8,128)(2,1)S(1)}, bf16[2,8,1008]{2,1,0:T(8,128)(2,1)}, u32[]{:S(2)}) copy-start(bf16[2,8,1008]{2,1,0:T(8,128)(2,1)} %slow_ref.1) | copy-start | bytes 96772
  5.5 0.7 %copy-start.5 = (bf16[2,512,8]{1,2,0:T(8,128)(2,1)S(1)}, bf16[2,512,8]{1,2,0:T(8,128)(2,1)}, u32[]{:S(2)}) copy-start(bf16[2,512,8]{1,2,0:T(8,128)(2,1)} %param.11) | copy-start | bytes 49156
where the time goes:
time: 65.6 us; the launch traced here: 65.2 us
  Pallas kernels  57.7 us (88%)
  local copies, waits for them, and re-layouts  6.2 us (9%)
  between operations  1.31 us (2%)
    pallas_call x1, Pallas kernels, body(): pl.pallas_call(kernel, out_shape=(jax.ShapeDtypeStruct((2, 16, 512), f32)...  57.7 us
    unnamed x16, local copies, waits for them, and re-layouts  6.2 us

commit v1 on v0

--- a/solution.py
+++ b/solution.py
@@ -43,13 +43,21 @@
 
 
 def kernel(
-    rhs_ref, sep_ref, inv_ref, low_ref, sinv_ref, slow_ref, live_ref, tgt_ref,
+    rhs_hbm, sep_hbm, inv_hbm, low_hbm, sinv_hbm, slow_hbm, tgt_hbm, live_ref,
     leaf_out, sep_out,
+    rhs_ref, sep_ref, inv_ref, low_ref, sinv_ref, slow_ref, tgt_ref, lsem,
     st, pk, m0, c0, c1, c2, c3, c4, zxs, zxr, eh, tt, p0, pis, pi4, rs_, vs, bs,
     m123, m4, m5, m6, i14, i5, i6, i7,
     s4, r4, s5, r5, s6, r6, s7, r7, xb7, xb6, xb5, sw5, rw5, sw6, rw6, w5o, w6o,
     lws, lwr, lwo, xo, xt, ssem, rsem,
 ):
+    loads = []
+    for j, (src, dst) in enumerate((
+        (rhs_hbm, rhs_ref), (low_hbm, low_ref), (sep_hbm, sep_ref), (slow_hbm, slow_ref),
+        (sinv_hbm, sinv_ref), (tgt_hbm, tgt_ref), (inv_hbm, inv_ref),
+    )):
+        loads.append(pltpu.make_async_copy(src, dst, lsem.at[j]))
+        loads[-1].start()
     leaf = lax.axis_index("leaf")
     x = lax.axis_index("rhs")
     c = lax.rem(leaf, 2)
@@ -88,6 +96,8 @@
         pending.append(out)
         return out
 
+    loads[0].wait()
+    loads[1].wait()
     live = live_ref[0]
     mask = iota((1, 512), 1) < live * 128
     zr = jnp.where(mask, rhs_ref[0], 0.0).astype(bf16)
@@ -100,6 +110,7 @@
     eh[...] = ehv
     zcat = jnp.concatenate([zr, zi], axis=1)
     st[:, 112:128] = mm_nt(ehv, zcat)
+    loads[2].wait()
     for level in range(7):
         st[0:8, 16 * level : 16 * level + 16] = sep_ref[0, level]
         st[8:16, 16 * level : 16 * level + 16] = sep_ref[1, level]
@@ -110,6 +121,8 @@
     zxr[x] = zxs[x]
     pk[:, 0:128] = jnp.zeros((16, 128), f32)
     pk[:, 1024:1152] = jnp.zeros((16, 128), f32)
+    loads[3].wait()
+    loads[4].wait()
     for part in range(2):
         pk[8 * part : 8 * part + 8, 16:1024] = slow_ref[part].astype(f32)
         pk[8 * part : 8 * part + 8, 1040:3072] = sinv_ref[part].astype(f32)
@@ -154,6 +167,7 @@
             send("t%d" % index, 0, buf.at[:, c], buf.at[:, c], dev(z, y, 1 - c, x))
         )
 
+    loads[5].wait()
     tgt = tgt_ref[...].astype(f32).astype(bf16)
     row = iota((256, 128), 0)
     col = iota((256, 128), 1)
@@ -314,6 +328,7 @@
     arrive("zx")
     zr4 = zxr[:, 0].reshape(64, 128)
     zi4 = zxr[:, 1].reshape(64, 128)
+    loads[6].wait()
     panel = inv_ref[...].reshape(256, 512)
     real = mm(jnp.concatenate([zr4, -zi4], axis=1), panel).reshape(4, 16, 512)
     imag = mm(jnp.concatenate([zi4, zr4], axis=1), panel).reshape(4, 16, 512)
@@ -384,6 +399,7 @@
 
 def body(leaf_rhs, sep_rhs, leaf_inv, leaf_low, sep_inv, sep_low, leaf_live, targets):
     vm = pl.BlockSpec(memory_space=pltpu.VMEM)
+    hb = pl.BlockSpec(memory_space=pltpu.HBM)
     sm = pl.BlockSpec(memory_space=pltpu.SMEM)
     V = pltpu.VMEM
     out_leaf, out_sep = pl.pallas_call(
@@ -392,9 +408,12 @@
             jax.ShapeDtypeStruct((2, 16, 512), f32),
             jax.ShapeDtypeStruct((2, 7, 8, 16), f32),
         ),
-        in_specs=[vm, vm, vm, vm, vm, vm, sm, vm],
+        in_specs=[hb, hb, hb, hb, hb, hb, hb, sm],
         out_specs=(vm, vm),
         scratch_shapes=[
+            V((2, 16, 512), f32), V((2, 7, 8, 16), f32), V((2, 128, 512), bf16),
+            V((2, 8, 512), bf16), V((2, 8, 2032), bf16), V((2, 8, 1008), bf16),
+            V((7, 128), jnp.int32), pltpu.SemaphoreType.DMA((7,)),
             V((16, 128), f32), V((16, 3072), f32), V((8, 2, 16, 128), bf16),
             V((8, 2, 16, 512), bf16), V((8, 2, 16, 256), bf16), V((8, 2, 16, 512), bf16),
             V((8, 2, 16, 1024), bf16), V((8, 2, 16, 768), bf16),
@@ -415,11 +434,11 @@
             pltpu.SemaphoreType.DMA((COPIES,)), pltpu.SemaphoreType.DMA((COPIES,)),
         ],
         compiler_params=pltpu.CompilerParams(
-            collective_id=0, has_side_effects=True, vmem_limit_bytes=40 * 2**20
+            collective_id=0, has_side_effects=True, vmem_limit_bytes=60 * 2**20
         ),
     )(
         leaf_rhs, sep_rhs.transpose(0, 2, 3, 1), leaf_inv, leaf_low.transpose(0, 2, 1),
-        sep_inv, sep_low, leaf_live, targets,
+        sep_inv, sep_low, targets, leaf_live,
     )
     return out_leaf, out_sep.transpose(0, 3, 1, 2)
 

time: 65.6 us -> 62 us (0.945)
  local copies, waits for them, and re-layouts: 6.2 us -> 2.12 us
  Pallas kernels: 57.7 us -> 58.4 us
    unnamed x16 -> x4, local copies, waits for them, and re-layouts: 6.2 us -> 2.12 us
    pallas_call x1, Pallas kernels: 57.7 us -> 58.4 us  [body(): pl.pallas_call(kernel, out_shape=(jax.ShapeDtypeStruct((2, 16, 512), f32)...]
where the time goes in v1:
time: 62 us; the launch traced here: 61.8 us
  Pallas kernels  58.4 us (94%)
  local copies, waits for them, and re-layouts  2.12 us (3%)
  between operations  1.3 us (2%)
    pallas_call x1, Pallas kernels, body(): pl.pallas_call(kernel, out_shape=(jax.ShapeDtypeStruct((2, 16, 512), f32)...  58.4 us
    unnamed x4, local copies, waits for them, and re-layouts  2.12 us

profile of v1, /device:TPU:2, one launch (start us, length us, event | category | flops | bytes accessed | tf_op | source)
XLA Modules:
  0.0 61.8 jit_solution(7784852983311514620)
XLA Ops:
  1.3 58.4 %shard_map.95 = (f32[2,16,512]{2,1,0:T(8,128)}, f32[2,7,8,16]{3,2,1,0:T(8,128)}) custom-call(f32[2,16,512]{2,1,0:T(8,128)} %rhs_hbm.1, f32[2,7,8,16]{3,2,1,0:T(8,128)} %bitcast.3, bf16[2,128,512]{2,1,0:T(8,128)(2,1)} %inv_hbm.1, bf16[2,8,512]{2,1,0:T(8,128)(2,1)} %bitcast.5, bf16[2,8,2032]{2,1,0:T(8,128)(2,1)} %sinv_hbm.1, bf16[2,8,1008]{2,1,0:T(8,128)(2,1)} %slow_hbm.1, ...), custom_call_target="tpu_custom_call" | custom-call | tf_op jit(solution)/shard_map/pallas_call | solution.py:405
  59.7 0.0 copy-start
  59.7 1.5 %copy.13 = f32[2,16,512]{2,1,0:T(8,128)} copy(f32[2,16,512]{2,1,0:T(8,128)} %get-tuple-element.8) | data formatting | bytes 131072
  61.2 0.0 copy-done
  61.2 0.6 %copy.14 = f32[2,16,7,8]{1,3,2,0:T(8,128)} copy(f32[2,16,7,8]{1,3,2,0:T(8,128)S(1)} %bitcast.4) | data formatting | bytes 14336
Async XLA Ops:
  59.7 1.5 %copy-start = (f32[2,7,8,16]{3,2,1,0:T(8,128)S(1)}, f32[2,7,8,16]{3,2,1,0:T(8,128)}, u32[]{:S(2)}) copy-start(f32[2,7,8,16]{3,2,1,0:T(8,128)} %get-tuple-element.5) | copy-start | bytes 21508

commit v2 on v1

v2 whole, which is shorter than its diff:
```python
import jax
import jax.numpy as jnp
from jax import lax
from jax.experimental import pallas as pl
from jax.experimental.pallas import tpu as pltpu
from jax.sharding import PartitionSpec as P

MESH = pl.DeviceIdType.MESH
bf16 = jnp.bfloat16
f32 = jnp.float32

COUNTS = dict(
    msg=15, zx=3, c0=7, c4=7, q1=1, q2=3, q3=7, c1=7, c2=7, c3=7, t0=1, t1=1, t2=1, t3=1, t4=1,
    h5=1, h6=3, h7=7, u4=1, u5=3, u6=7, d6=3, d5=1, g6=7, g5=3, g4=1, lw=3,
)
FIRST = {}
_total = 0
for _name, _count in COUNTS.items():
    FIRST[_name] = _total
    _total += _count
COPIES = _total


def mm(a, b):
    return jnp.dot(a, b, preferred_element_type=f32)


def mm_nt(a, b):
    return lax.dot_general(a, b, (((1,), (1,)), ((), ())), preferred_element_type=f32)


def flip(value, mask):
    out = value
    for bit in range(3):
        if mask >> bit & 1:
            here = lax.rem(lax.div(value, 1 << bit), 2)
            out = out + (1 - 2 * here) * (1 << bit)
    return out


def iota(shape, axis):
    return lax.broadcasted_iota(jnp.int32, shape, axis)


def hot(test):
    return test.astype(f32).astype(bf16)


def kernel(
    rhs_hbm, sep_hbm, inv_hbm, low_hbm, sinv_hbm, slow_hbm, tgt_hbm, live_ref, tgs,
    leaf_out, sep_out,
    rhs_ref, sep_ref, inv_ref, low_ref, sinv_ref, slow_ref, tgt_ref, lsem,
    st, pk, m0, c0, c4, p1, p2, p3, c1, c2, c3, zxs, zxr, eh, dl_, p0, pis, rs_, vs,
    m123, b4, b5, b6, b7, n5, n6, n7, i14, i5, i6, h5, h6, h7, u4g, u5g, u6g,
    wq6, wq5, d6s, d6r, d5s, d5r, g6g, g5g, g4g, lws, lwr, lwo, xo, xt, ssem, rsem,
):
    loads = []
    for j, (src, dst) in enumerate((
        (rhs_hbm, rhs_ref), (low_hbm, low_ref), (sep_hbm, sep_ref), (slow_hbm, slow_ref),
        (sinv_hbm, sinv_ref), (tgt_hbm, tgt_ref), (inv_hbm, inv_ref),
    )):
        loads.append(pltpu.make_async_copy(src, dst, lsem.at[j]))
        loads[-1].start()
    leaf = lax.axis_index("leaf")
    x = lax.axis_index("rhs")
    c = lax.rem(leaf, 2)
    y = lax.rem(lax.div(leaf, 2), 8)
    z = lax.div(leaf, 16)
    dl = lax.rem(leaf, 16)
    zq = lax.rem(z, 4)
    zp = lax.rem(z, 2)
    quad = z - zq
    pair = z - zp

    def dev(zz, yy, cc, xx):
        return (zz * 16 + yy * 2 + cc, xx)

    layer = [(k >> 1, k & 1) for k in range(1, 16)]
    barrier = pltpu.get_barrier_semaphore()

    def greet(device):
        pl.semaphore_signal(barrier, inc=1, device_id=device, device_id_type=MESH)

    for ky, kc in layer:
        greet(dev(z, flip(y, ky), flip(c, kc), x))
    for k in range(1, 8):
        greet(dev(flip(z, k), y, c, x))
    for k in range(1, 4):
        greet(dev(z, y, c, flip(x, k)))

    pending = []
    got = {name: [] for name in COUNTS}

    def send(name, src, dst, device):
        index = FIRST[name] + len(got[name])
        out = pltpu.make_async_remote_copy(
            src_ref=src, dst_ref=dst, send_sem=ssem.at[index], recv_sem=rsem.at[index],
            device_id=device, device_id_type=MESH,
        )
        out.start()
        pending.append(out)
        got[name].append(out)

    def arrive(name):
        for one in got[name]:
            one.wait_recv()

    def scatter(name, buf):
        for k in range(1, 8):
            send(name, buf.at[y, c], buf.at[y, c], dev(z, flip(y, k), c, x))

    def twin(name, tag, buf):
        arrive(name)
        send(tag, buf.at[:, c], buf.at[:, c], dev(z, y, 1 - c, x))

    def along(name, count, buf, slot):
        for k in range(1, count):
            send(name, buf.at[slot], buf.at[slot], dev(flip(z, k), y, c, x))

    loads[0].wait()
    loads[1].wait()
    live = live_ref[0]
    mask = iota((1, 512), 1) < live * 128
    zr = jnp.where(mask, rhs_ref[0], 0.0).astype(bf16)
    zi = jnp.where(mask, rhs_ref[1], 0.0).astype(bf16)
    er = low_ref[0].astype(f32)
    ei = low_ref[1].astype(f32)
    ehv = jnp.concatenate(
        [jnp.concatenate([er, -ei], axis=1), jnp.concatenate([ei, er], axis=1)], axis=0
    ).astype(bf16)
    eh[...] = ehv
    zcat = jnp.concatenate([zr, zi], axis=1)
    st[:, 112:128] = mm_nt(ehv, zcat)
    loads[2].wait()
    for level in range(7):
        st[0:8, 16 * level : 16 * level + 16] = sep_ref[0, level]
        st[8:16, 16 * level : 16 * level + 16] = sep_ref[1, level]
    m0[y, c] = st[...].astype(bf16)
    pk[:, 0:128] = jnp.zeros((16, 128), f32)
    pk[:, 1024:1152] = jnp.zeros((16, 128), f32)
    loads[3].wait()
    loads[4].wait()
    for part in range(2):
        pk[8 * part : 8 * part + 8, 16:1024] = slow_ref[part].astype(f32)
        pk[8 * part : 8 * part + 8, 1040:3072] = sinv_ref[part].astype(f32)
    c0[y, c, :, 0:256] = pk[:, 0:256].astype(bf16)
    c0[y, c, :, 256:512] = pk[:, 1024:1280].astype(bf16)
    c4[y, c] = pk[:, 1280:2048].astype(bf16)
    for q in range(4):
        zxs[q, 0] = zr[:, 128 * q : 128 * q + 128]
        zxs[q, 1] = zi[:, 128 * q : 128 * q + 128]
    zxr[x] = zxs[x]
    for t in range(2):
        p1[t] = pk[:, 256 + 128 * t : 384 + 128 * t].astype(bf16)
    for t in range(4):
        p2[t] = pk[:, 512 + 128 * t : 640 + 128 * t].astype(bf16)
    c1[y, c, zp] = p1[zp]
    c2[y, c, zq] = p2[zq]
    loads[5].wait()
    tgt = tgt_ref[...].astype(f32).astype(bf16)
    spot = iota((128, 1024), 1)
    wide = mm(tgt, hot(iota((128, 1024), 0) == spot // 8))
    place = 8.0 * wide[6:7] + (iota((1, 1024), 1) % 8).astype(f32)
    top_rows = pk[:, 2048:3072].astype(bf16)
    down = iota((1024, 256), 0).astype(f32)
    for t in range(4):
        moved = mm(top_rows, hot(down == place[:, 256 * t : 256 * t + 256])).astype(bf16)
        p3[2 * t] = moved[:, 0:128]
        p3[2 * t + 1] = moved[:, 128:256]
    c3[y, c, z] = p3[z]

    pl.semaphore_wait(barrier, 25)

    for ky, kc in layer:
        send("msg", m0.at[y, c], m0.at[y, c], dev(z, flip(y, ky), flip(c, kc), x))
    scatter("c0", c0)
    send("q1", p1.at[1 - zp], c1.at[y, c, zp], dev(flip(z, 1), y, c, x))
    for k in range(1, 4):
        send("q2", p2.at[flip(zq, k)], c2.at[y, c, zq], dev(flip(z, k), y, c, x))
    for k in range(1, 8):
        send("q3", p3.at[flip(z, k)], c3.at[y, c, z], dev(flip(z, k), y, c, x))
    for k in range(1, 4):
        send("zx", zxs.at[flip(x, k)], zxr.at[x], dev(z, y, c, flip(x, k)))

    lane16 = (iota((1, 256), 1) % 16).astype(f32)
    for s in range(8):
        pick = iota((128, 256), 0) == 16 * s + iota((128, 256), 1) // 16
        dl_[s, 0:7] = 16.0 * mm(tgt, hot(pick)) + lane16
    down = iota((256, 256), 0).astype(f32)

    def route(level, source, slab):
        shift = jnp.asarray(256 * slab, jnp.int32).astype(f32)
        return hot(down + shift == dl_[source][level : level + 1])

    p0[...] = hot(down == dl_[z][0:1] + (iota((1, 256), 1) // 32 * 32).astype(f32))
    lane = iota((1, 256), 1)
    pick = iota((128, 256), 0) == 16 * z + iota((128, 256), 1) % 128 // 8
    inner = (lane // 128 * 8 + lane % 8).astype(f32)
    old = 16.0 * mm(tgt, hot(pick)) + inner
    for level in range(1, 4):
        base = (lane % 128 // 8 // (2 << level) * (2 << level) * 16).astype(f32)
        pis[level - 1] = hot(down == old[level : level + 1] + base)
    rown = iota((256, 1), 0)
    natural = hot(iota((256, 256), 1) == rown % 128 // 8 * 16 + rown // 128 * 8 + rown % 8)
    sign_row = (1 - 2 * (iota((256, 1), 0) // 8 % 2)).astype(f32)
    sign_lane = (1 - 2 * (lane // 8 % 2)).astype(f32)

    def embed(raw):
        parts = raw.reshape(16, 2, 8, 128)
        swapped = jnp.concatenate([parts[:, 1:2], parts[:, 0:1]], axis=1).reshape(256, 128)
        return jnp.concatenate([raw * sign_row, swapped], axis=1).astype(bf16)

    def square(raw):
        return mm(embed(raw.reshape(256, 128).astype(f32)), natural).astype(bf16)

    def small(raw, level):
        size = 8 << level
        at = iota((128, 128), 0)
        to = iota((128, 128), 1)
        repeat = hot(at == size + to % size)
        spread = mm(raw, repeat)
        front = iota((256, 128), 0) // (16 << level) == iota((256, 128), 1) // size
        return embed(jnp.where(front, spread, 0.0))

    def blocks(ref, s):
        return ref[pl.ds(16 * s, 16)].reshape(256, 256)

    arrive("msg")
    flipped = jnp.transpose(m0[...].reshape(256, 128).astype(f32))
    rs_[...] = flipped
    u = mm_nt(flipped[112:128].astype(bf16), p0[...])
    v = (flipped[0:16] - u).astype(bf16)
    vs[0] = v
    twin("c0", "t0", c0)
    arrive("q1")
    scatter("c1", c1)
    arrive("q2")
    scatter("c2", c2)
    arrive("t0")
    raw0 = c0[:, :, :, 0:128].reshape(256, 128)
    for level in range(1, 4):
        m123[level - 1] = mm_nt(small(raw0, level), pis[level - 1]).astype(bf16)
        u = mm(v, m123[level - 1])
        v = (rs_[16 * level : 16 * level + 16] - u).astype(bf16)
        vs[level] = v
    b4[...] = square(c0[:, :, :, 128:256])
    own = mm(v, b4[...]).astype(bf16)
    u4g[zp] = own
    along("u4", 2, u4g, zp)
    h5[zp] = rs_[64:80].astype(bf16)
    h6[zq] = rs_[80:96].astype(bf16)
    h7[z] = rs_[96:112].astype(bf16)
    along("h5", 2, h5, zp)
    along("h6", 4, h6, zq)
    along("h7", 8, h7, z)
    arrive("q3")
    scatter("c3", c3)
    scatter("c4", c4)

    twin("c1", "t1", c1)
    arrive("t1")
    for s in range(2):
        b5[16 * s : 16 * s + 16] = square(c1[:, :, s]).reshape(16, 16, 256)

    def move(level, first, source, target):
        def step(i, carry):
            target[i] = source[tgs[level, first + i]]
            return carry
        return step

    lax.fori_loop(0, 32, move(4, 16 * pair, b5, n5), 0, unroll=8)
    arrive("h5")
    u = mm(h5[0], blocks(b5, 0)) + mm(h5[1], blocks(b5, 1)) - mm(own, blocks(n5, zp))
    arrive("u4")
    u = u - mm(u4g[1 - zp], blocks(n5, 1 - zp))
    own = u.astype(bf16)
    u5g[zq] = own
    along("u5", 4, u5g, zq)

    twin("c2", "t2", c2)
    arrive("t2")
    for s in range(4):
        b6[16 * s : 16 * s + 16] = square(c2[:, :, s]).reshape(16, 16, 256)
    lax.fori_loop(0, 64, move(5, 16 * quad, b6, n6), 0, unroll=8)
    arrive("h6")
    u = -mm(own, blocks(n6, zq))
    for s in range(4):
        u = u + mm(h6[s], blocks(b6, s))
    for k in range(1, 4):
        got["u5"][k - 1].wait_recv()
        u = u - mm(u5g[flip(zq, k)], blocks(n6, flip(zq, k)))
    own = u.astype(bf16)
    u6g[z] = own
    along("u6", 8, u6g, z)

    twin("c3", "t3", c3)
    arrive("t3")
    for s in range(8):
        b7[16 * s : 16 * s + 16] = square(c3[:, :, s]).reshape(16, 16, 256)
    lax.fori_loop(0, 128, move(6, 0, b7, n7), 0, unroll=8)
    arrive("h7")
    u = -mm(own, blocks(n7, z))
    for s in range(8):
        u = u + mm(h7[s], blocks(b7, s))

    twin("c4", "t4", c4)
    arrive("t4")
    v5 = rs_[64:80]
    for s in range(2):
        i5[s] = square(c4[:, :, :, 128 * s : 128 * s + 128])
        v5 = v5 - mm_nt(u4g[s], route(4, pair + s, zp))
    v5 = v5.astype(bf16)
    v6 = rs_[80:96]
    for s in range(4):
        i6[s] = square(c4[:, :, :, 256 + 128 * s : 384 + 128 * s])
        v6 = v6 - mm_nt(u5g[s], route(5, quad + s, zq))
    v6 = v6.astype(bf16)
    w6 = [mm(v6, i6[s]).astype(bf16) for s in range(4)]
    for s in range(4):
        total = mm(w6[0], route(5, quad + s, 0))
        for t in range(1, 4):
            total = total + mm(w6[t], route(5, quad + s, t))
        wq6[s] = total * sign_lane

    for k in range(1, 8):
        got["u6"][k - 1].wait_recv()
        u = u - mm(u6g[flip(z, k)], blocks(n7, flip(z, k)))
    own = (u * sign_lane).astype(bf16)

    for k in range(1, 4):
        t = flip(zq, k)
        d6s[k - 1] = (wq6[t] - mm_nt(own, blocks(n6, t))).astype(bf16)
        send("d6", d6s.at[k - 1], d6r.at[k - 1], dev(flip(z, k), y, c, x))
    below = wq6[zq] - mm_nt(own, blocks(n6, zq))
    g6g[z] = own
    along("g6", 8, g6g, z)

    w5 = [mm(v5, i5[s]).astype(bf16) for s in range(2)]
    for s in range(2):
        wq5[s] = sign_lane * (
            mm(w5[0], route(4, pair + s, 0)) + mm(w5[1], route(4, pair + s, 1))
        )
    arrive("d6")
    for k in range(3):
        below = below + d6r[k].astype(f32)
    own = below.astype(bf16)
    d5s[...] = (wq5[1 - zp] - mm_nt(own, blocks(n5, 1 - zp))).astype(bf16)
    send("d5", d5s, d5r, dev(flip(z, 1), y, c, x))
    below = wq5[zp] - mm_nt(own, blocks(n5, zp))
    g5g[zq] = own
    along("g5", 4, g5g, zq)

    arrive("zx")
    loads[6].wait()
    zr4 = zxr[:, 0].reshape(64, 128)
    zi4 = zxr[:, 1].reshape(64, 128)
    panel = inv_ref[...].reshape(256, 512)
    real = mm(jnp.concatenate([zr4, -zi4], axis=1), panel).reshape(4, 16, 512)
    imag = mm(jnp.concatenate([zi4, zr4], axis=1), panel).reshape(4, 16, 512)
    lwo[:, 0] = real
    lwo[:, 1] = imag
    lws[:, 0] = real.astype(bf16)
    lws[:, 1] = imag.astype(bf16)
    for k in range(1, 4):
        send("lw", lws.at[flip(x, k)], lwr.at[k - 1], dev(z, y, c, flip(x, k)))
    rawi = c0[:, :, :, 256:384].reshape(256, 128)
    for level in range(1, 4):
        i14[level - 1] = mm(small(rawi, level), natural).astype(bf16)
    i14[3] = square(c0[:, :, :, 384:512])
    for level in range(1, 5):
        xo[16 * level - 16 : 16 * level] = mm(vs[level - 1], i14[level - 1]) * sign_lane

    arrive("d5")
    own = (below + d5r[...].astype(f32)).astype(bf16)
    g4g[zp] = own
    along("g4", 2, g4g, zp)
    now = xo[48:64] - mm_nt(own, b4[...])
    xo[48:64] = now
    for level in range(3, 0, -1):
        now = xo[16 * level - 16 : 16 * level] - mm_nt(now.astype(bf16), m123[level - 1])
        xo[16 * level - 16 : 16 * level] = now
    parent = 16 * (dl - c + tgs[0, leaf])
    chosen = hot(iota((16, 256), 1) == parent + iota((16, 256), 0))
    back = mm_nt(now.astype(bf16), chosen).astype(bf16)
    less = mm(back, eh[...])
    arrive("lw")
    mine = lwo[x]
    for k in range(3):
        mine = mine + lwr[k].astype(f32)
    leaf_out[0] = jnp.where(mask, mine[0] - less[:, 0:512], 0.0)
    leaf_out[1] = jnp.where(mask, mine[1] + less[:, 512:1024], 0.0)

    xt[...] = jnp.transpose(xo[...])
    start = pl.multiple_of(dl * 16, 16)
    turned = xt[pl.ds(start, 16), :]
    for level in range(4):
        sep_out[0, level] = turned[0:8, 16 * level : 16 * level + 16]
        sep_out[1, level] = -turned[8:16, 16 * level : 16 * level + 16]
    arrive("g6")
    arrive("g5")
    arrive("g4")
    for level, size, first, ref in ((7, 8, 0, g6g), (6, 4, quad, g5g), (5, 2, pair, g4g)):
        want = (16 * (leaf - 16 * first) + iota((16, 256), 0)).astype(f32)
        block = jnp.zeros((16, 16), f32)
        for s in range(size):
            block = block + mm_nt(hot(want == dl_[first + s][level - 1 : level]), ref[s])
        sep_out[0, level - 1] = block[0:8]
        sep_out[1, level - 1] = -block[8:16]

    for one in pending:
        one.wait_send()


def body(leaf_rhs, sep_rhs, leaf_inv, leaf_low, sep_inv, sep_low, leaf_live, targets):
    vm = pl.BlockSpec(memory_space=pltpu.VMEM)
    hb = pl.BlockSpec(memory_space=pltpu.HBM)
    sm = pl.BlockSpec(memory_space=pltpu.SMEM)
    V = pltpu.VMEM

    def rows(*lead):
        return V(lead + (16, 256), bf16)

    def squares(count):
        return V((count, 256, 256), bf16)

    out_leaf, out_sep = pl.pallas_call(
        kernel,
        out_shape=(
            jax.ShapeDtypeStruct((2, 16, 512), f32),
            jax.ShapeDtypeStruct((2, 7, 8, 16), f32),
        ),
        in_specs=[hb, hb, hb, hb, hb, hb, hb, sm, sm],
        out_specs=(vm, vm),
        scratch_shapes=[
            V((2, 16, 512), f32), V((2, 7, 8, 16), f32), V((2, 128, 512), bf16),
            V((2, 8, 512), bf16), V((2, 8, 2032), bf16), V((2, 8, 1008), bf16),
            V((7, 128), jnp.int32), pltpu.SemaphoreType.DMA((7,)),
            V((16, 128), f32), V((16, 3072), f32), V((8, 2, 16, 128), bf16),
            V((8, 2, 16, 512), bf16), V((8, 2, 16, 768), bf16),
            V((2, 16, 128), bf16), V((4, 16, 128), bf16), V((8, 16, 128), bf16),
            V((8, 2, 2, 16, 128), bf16), V((8, 2, 4, 16, 128), bf16), V((8, 2, 8, 16, 128), bf16),
            V((4, 2, 16, 128), bf16), V((4, 2, 16, 128), bf16), V((16, 1024), bf16),
            V((8, 8, 256), f32), V((256, 256), bf16), squares(3),
            V((128, 256), f32), rows(4),
            squares(3), V((256, 256), bf16), rows(32), rows(64), rows(128),
            rows(32), rows(64), rows(128), squares(4), squares(2), squares(4),
            rows(2), rows(4), rows(8), rows(2), rows(4), rows(8),
            V((4, 16, 256), f32), V((2, 16, 256), f32), rows(3), rows(3), rows(), rows(),
            rows(8), rows(4), rows(2),
            V((4, 2, 16, 512), bf16), V((3, 2, 16, 512), bf16), V((4, 2, 16, 512), f32),
            V((64, 256), f32), V((256, 64), f32),
            pltpu.SemaphoreType.DMA((COPIES,)), pltpu.SemaphoreType.DMA((COPIES,)),
        ],
        compiler_params=pltpu.CompilerParams(
            collective_id=0, has_side_effects=True, vmem_limit_bytes=60 * 2**20
        ),
    )(
        leaf_rhs, sep_rhs.transpose(0, 2, 3, 1), leaf_inv, leaf_low.transpose(0, 2, 1),
        sep_inv, sep_low, targets, leaf_live, targets,
    )
    return out_leaf, out_sep.transpose(0, 3, 1, 2)


def solution(mesh):
    placed = (
        P(None, "rhs", "leaf"),
        P(None, "rhs", None, "leaf"),
        P(None, "rhs", "leaf"),
        P(None, None, "leaf"),
        P(None, None, "leaf"),
        P(None, None, "leaf"),
        P("leaf"),
        P(),
    )
    return jax.shard_map(
        body,
        mesh=mesh,
        in_specs=placed,
        out_specs=(P(None, "rhs", "leaf"), P(None, "rhs", None, "leaf")),
        check_vma=False,
    )
```

time: 62 us -> 56.7 us (0.915)
  the two profiles are of different devices: /device:TPU:2 before, /device:TPU:1 now
where the time goes in v2:
time: 56.7 us; the launch traced here: 56.4 us
  Pallas kernels  53 us (93%)
  local copies, waits for them, and re-layouts  2.12 us (4%)
  between operations  1.3 us (2%)
    pallas_call x1, Pallas kernels, body(): pl.pallas_call(kernel, out_shape=(jax.ShapeDtypeStruct((2, 16, 512), f32)...  53 us
    unnamed x4, local copies, waits for them, and re-layouts  2.12 us

profile of v2, /device:TPU:1, one launch (start us, length us, event | category | flops | bytes accessed | tf_op | source)
XLA Modules:
  0.0 56.4 jit_solution(17130555815378330498)
XLA Ops:
  1.3 53.0 %shard_map.95 = (f32[2,16,512]{2,1,0:T(8,128)}, f32[2,7,8,16]{3,2,1,0:T(8,128)}) custom-call(f32[2,16,512]{2,1,0:T(8,128)} %rhs_hbm.1, f32[2,7,8,16]{3,2,1,0:T(8,128)} %bitcast.3, bf16[2,128,512]{2,1,0:T(8,128)(2,1)} %inv_hbm.1, bf16[2,8,512]{2,1,0:T(8,128)(2,1)} %bitcast.5, bf16[2,8,2032]{2,1,0:T(8,128)(2,1)} %sinv_hbm.1, bf16[2,8,1008]{2,1,0:T(8,128)(2,1)} %slow_hbm.1, ...), custom_call_target="tpu_custom_call" | custom-call | tf_op jit(solution)/shard_map/pallas_call | solution.py:426
  54.3 0.0 copy-start
  54.3 1.5 %copy.13 = f32[2,16,512]{2,1,0:T(8,128)} copy(f32[2,16,512]{2,1,0:T(8,128)} %get-tuple-element.8) | data formatting | bytes 131072
  55.8 0.0 copy-done
  55.8 0.6 %copy.14 = f32[2,16,7,8]{1,3,2,0:T(8,128)} copy(f32[2,16,7,8]{1,3,2,0:T(8,128)S(1)} %bitcast.4) | data formatting | bytes 14336
Async XLA Ops:
  54.3 1.5 %copy-start = (f32[2,7,8,16]{3,2,1,0:T(8,128)S(1)}, f32[2,7,8,16]{3,2,1,0:T(8,128)}, u32[]{:S(2)}) copy-start(f32[2,7,8,16]{3,2,1,0:T(8,128)} %get-tuple-element.5) | copy-start | bytes 21508

commit v3 on v2

--- a/solution.py
+++ b/solution.py
@@ -11,7 +11,7 @@
 
 COUNTS = dict(
     msg=15, zx=3, c0=7, c4=7, q1=1, q2=3, q3=7, c1=7, c2=7, c3=7, t0=1, t1=1, t2=1, t3=1, t4=1,
-    h5=1, h6=3, h7=7, u4=1, u5=3, u6=7, d6=3, d5=1, g6=7, g5=3, g4=1, lw=3,
+    x2=3, x3=3, x4=3, h=7, u4=1, u5=3, u6=7, d6=3, d5=1, g6=7, g5=3, lw=3,
 )
 FIRST = {}
 _total = 0
@@ -50,8 +50,8 @@
     rhs_hbm, sep_hbm, inv_hbm, low_hbm, sinv_hbm, slow_hbm, tgt_hbm, live_ref, tgs,
     leaf_out, sep_out,
     rhs_ref, sep_ref, inv_ref, low_ref, sinv_ref, slow_ref, tgt_ref, lsem,
-    st, pk, m0, c0, c4, p1, p2, p3, c1, c2, c3, zxs, zxr, eh, dl_, p0, pis, rs_, vs,
-    m123, b4, b5, b6, b7, n5, n6, n7, i14, i5, i6, h5, h6, h7, u4g, u5g, u6g,
+    st, pk, m0, c0, c4, p1, p2, p3, p4, z2, z3, c1, c2, c3, zxs, zxr, eh, dl_, p0, pis, rs_, vs,
+    m123, b4, b5, b6, b7, n5, n6, n7, i14, i5, i6, hh, u4g, u5g, u6g,
     wq6, wq5, d6s, d6r, d5s, d5r, g6g, g5g, g4g, lws, lwr, lwo, xo, xt, ssem, rsem,
 ):
     loads = []
@@ -108,6 +108,15 @@
     def scatter(name, buf):
         for k in range(1, 8):
             send(name, buf.at[y, c], buf.at[y, c], dev(z, flip(y, k), c, x))
+
+    def quarter(name, buf):
+        for k in range(1, 8):
+            send(name, buf.at[y, c, x], buf.at[y, c, x], dev(z, flip(y, k), c, x))
+
+    def planes(name, tag, buf):
+        arrive(name)
+        for k in range(1, 4):
+            send(tag, buf.at[:, c, x], buf.at[:, c, x], dev(z, y, c, flip(x, k)))
 
     def twin(name, tag, buf):
         arrive(name)
@@ -143,9 +152,10 @@
     for part in range(2):
         pk[8 * part : 8 * part + 8, 16:1024] = slow_ref[part].astype(f32)
         pk[8 * part : 8 * part + 8, 1040:3072] = sinv_ref[part].astype(f32)
-    c0[y, c, :, 0:256] = pk[:, 0:256].astype(bf16)
-    c0[y, c, :, 256:512] = pk[:, 1024:1280].astype(bf16)
-    c4[y, c] = pk[:, 1280:2048].astype(bf16)
+    c0[y, c] = pk[:, 0:256].astype(bf16)
+    for t in range(4):
+        p4[t] = pk[:, 1024 + 256 * t : 1280 + 256 * t].astype(bf16)
+    c4[y, c, x] = p4[x]
     for q in range(4):
         zxs[q, 0] = zr[:, 128 * q : 128 * q + 128]
         zxs[q, 1] = zi[:, 128 * q : 128 * q + 128]
@@ -155,7 +165,7 @@
     for t in range(4):
         p2[t] = pk[:, 512 + 128 * t : 640 + 128 * t].astype(bf16)
     c1[y, c, zp] = p1[zp]
-    c2[y, c, zq] = p2[zq]
+    z2[zq] = p2[zq]
     loads[5].wait()
     tgt = tgt_ref[...].astype(f32).astype(bf16)
     spot = iota((128, 1024), 1)
@@ -167,7 +177,7 @@
         moved = mm(top_rows, hot(down == place[:, 256 * t : 256 * t + 256])).astype(bf16)
         p3[2 * t] = moved[:, 0:128]
         p3[2 * t + 1] = moved[:, 128:256]
-    c3[y, c, z] = p3[z]
+    z3[lax.div(z, 2), zp] = p3[z]
 
     pl.semaphore_wait(barrier, 25)
 
@@ -176,9 +186,10 @@
     scatter("c0", c0)
     send("q1", p1.at[1 - zp], c1.at[y, c, zp], dev(flip(z, 1), y, c, x))
     for k in range(1, 4):
-        send("q2", p2.at[flip(zq, k)], c2.at[y, c, zq], dev(flip(z, k), y, c, x))
+        send("q2", p2.at[flip(zq, k)], z2.at[zq], dev(flip(z, k), y, c, x))
     for k in range(1, 8):
-        send("q3", p3.at[flip(z, k)], c3.at[y, c, z], dev(flip(z, k), y, c, x))
+        send("q3", p3.at[flip(z, k)], z3.at[lax.div(z, 2), zp], dev(flip(z, k), y, c, x))
+    quarter("c4", c4)
     for k in range(1, 4):
         send("zx", zxs.at[flip(x, k)], zxr.at[x], dev(z, y, c, flip(x, k)))
 
@@ -235,7 +246,8 @@
     arrive("q1")
     scatter("c1", c1)
     arrive("q2")
-    scatter("c2", c2)
+    c2[y, c, x] = z2[x]
+    quarter("c2", c2)
     arrive("t0")
     raw0 = c0[:, :, :, 0:128].reshape(256, 128)
     for level in range(1, 4):
@@ -247,109 +259,18 @@
     own = mm(v, b4[...]).astype(bf16)
     u4g[zp] = own
     along("u4", 2, u4g, zp)
-    h5[zp] = rs_[64:80].astype(bf16)
-    h6[zq] = rs_[80:96].astype(bf16)
-    h7[z] = rs_[96:112].astype(bf16)
-    along("h5", 2, h5, zp)
-    along("h6", 4, h6, zq)
-    along("h7", 8, h7, z)
+    hh[z, 0] = rs_[96:112].astype(bf16)
+    hh[z, 1] = rs_[80:96].astype(bf16)
+    hh[z, 2] = rs_[64:80].astype(bf16)
+    for k in range(1, 8):
+        part = pl.ds(0, 3 if k < 2 else 2 if k < 4 else 1)
+        send("h", hh.at[z, part], hh.at[z, part], dev(flip(z, k), y, c, x))
     arrive("q3")
-    scatter("c3", c3)
-    scatter("c4", c4)
+    c3[y, c, x] = z3[x]
+    quarter("c3", c3)
 
     twin("c1", "t1", c1)
-    arrive("t1")
-    for s in range(2):
-        b5[16 * s : 16 * s + 16] = square(c1[:, :, s]).reshape(16, 16, 256)
-
-    def move(level, first, source, target):
-        def step(i, carry):
-            target[i] = source[tgs[level, first + i]]
-            return carry
-        return step
-
-    lax.fori_loop(0, 32, move(4, 16 * pair, b5, n5), 0, unroll=8)
-    arrive("h5")
-    u = mm(h5[0], blocks(b5, 0)) + mm(h5[1], blocks(b5, 1)) - mm(own, blocks(n5, zp))
-    arrive("u4")
-    u = u - mm(u4g[1 - zp], blocks(n5, 1 - zp))
-    own = u.astype(bf16)
-    u5g[zq] = own
-    along("u5", 4, u5g, zq)
-
-    twin("c2", "t2", c2)
-    arrive("t2")
-    for s in range(4):
-        b6[16 * s : 16 * s + 16] = square(c2[:, :, s]).reshape(16, 16, 256)
-    lax.fori_loop(0, 64, move(5, 16 * quad, b6, n6), 0, unroll=8)
-    arrive("h6")
-    u = -mm(own, blocks(n6, zq))
-    for s in range(4):
-        u = u + mm(h6[s], blocks(b6, s))
-    for k in range(1, 4):
-        got["u5"][k - 1].wait_recv()
-        u = u - mm(u5g[flip(zq, k)], blocks(n6, flip(zq, k)))
-    own = u.astype(bf16)
-    u6g[z] = own
-    along("u6", 8, u6g, z)
-
-    twin("c3", "t3", c3)
-    arrive("t3")
-    for s in range(8):
-        b7[16 * s : 16 * s + 16] = square(c3[:, :, s]).reshape(16, 16, 256)
-    lax.fori_loop(0, 128, move(6, 0, b7, n7), 0, unroll=8)
-    arrive("h7")
-    u = -mm(own, blocks(n7, z))
-    for s in range(8):
-        u = u + mm(h7[s], blocks(b7, s))
-
-    twin("c4", "t4", c4)
-    arrive("t4")
-    v5 = rs_[64:80]
-    for s in range(2):
-        i5[s] = square(c4[:, :, :, 128 * s : 128 * s + 128])
-        v5 = v5 - mm_nt(u4g[s], route(4, pair + s, zp))
-    v5 = v5.astype(bf16)
-    v6 = rs_[80:96]
-    for s in range(4):
-        i6[s] = square(c4[:, :, :, 256 + 128 * s : 384 + 128 * s])
-        v6 = v6 - mm_nt(u5g[s], route(5, quad + s, zq))
-    v6 = v6.astype(bf16)
-    w6 = [mm(v6, i6[s]).astype(bf16) for s in range(4)]
-    for s in range(4):
-        total = mm(w6[0], route(5, quad + s, 0))
-        for t in range(1, 4):
-            total = total + mm(w6[t], route(5, quad + s, t))
-        wq6[s] = total * sign_lane
-
-    for k in range(1, 8):
-        got["u6"][k - 1].wait_recv()
-        u = u - mm(u6g[flip(z, k)], blocks(n7, flip(z, k)))
-    own = (u * sign_lane).astype(bf16)
-
-    for k in range(1, 4):
-        t = flip(zq, k)
-        d6s[k - 1] = (wq6[t] - mm_nt(own, blocks(n6, t))).astype(bf16)
-        send("d6", d6s.at[k - 1], d6r.at[k - 1], dev(flip(z, k), y, c, x))
-    below = wq6[zq] - mm_nt(own, blocks(n6, zq))
-    g6g[z] = own
-    along("g6", 8, g6g, z)
-
-    w5 = [mm(v5, i5[s]).astype(bf16) for s in range(2)]
-    for s in range(2):
-        wq5[s] = sign_lane * (
-            mm(w5[0], route(4, pair + s, 0)) + mm(w5[1], route(4, pair + s, 1))
-        )
-    arrive("d6")
-    for k in range(3):
-        below = below + d6r[k].astype(f32)
-    own = below.astype(bf16)
-    d5s[...] = (wq5[1 - zp] - mm_nt(own, blocks(n5, 1 - zp))).astype(bf16)
-    send("d5", d5s, d5r, dev(flip(z, 1), y, c, x))
-    below = wq5[zp] - mm_nt(own, blocks(n5, zp))
-    g5g[zq] = own
-    along("g5", 4, g5g, zq)
-
+    planes("c4", "x4", c4)
     arrive("zx")
     loads[6].wait()
     zr4 = zxr[:, 0].reshape(64, 128)
@@ -363,17 +284,126 @@
     lws[:, 1] = imag.astype(bf16)
     for k in range(1, 4):
         send("lw", lws.at[flip(x, k)], lwr.at[k - 1], dev(z, y, c, flip(x, k)))
-    rawi = c0[:, :, :, 256:384].reshape(256, 128)
+    planes("c2", "x2", c2)
+    arrive("t1")
+    for s in range(2):
+        b5[16 * s : 16 * s + 16] = square(c1[:, :, s]).reshape(16, 16, 256)
+
+    def move(level, first, source, target):
+        def step(i, carry):
+            target[i] = source[tgs[level, first + i]]
+            return carry
+        return step
+
+    lax.fori_loop(0, 32, move(4, 16 * pair, b5, n5), 0, unroll=8)
+    got["h"][0].wait_recv()
+    u = -mm(own, blocks(n5, zp))
+    for s in range(2):
+        u = u + mm(hh[pair + s, 2], blocks(b5, s))
+    arrive("u4")
+    u = u - mm(u4g[1 - zp], blocks(n5, 1 - zp))
+    own = u.astype(bf16)
+    u5g[zq] = own
+    along("u5", 4, u5g, zq)
+
+    twin("x2", "t2", c2)
+    planes("c3", "x3", c3)
+    arrive("t2")
+    for s in range(4):
+        b6[16 * s : 16 * s + 16] = square(c2[:, :, s]).reshape(16, 16, 256)
+    lax.fori_loop(0, 64, move(5, 16 * quad, b6, n6), 0, unroll=8)
+    got["h"][1].wait_recv()
+    got["h"][2].wait_recv()
+    u = -mm(own, blocks(n6, zq))
+    for s in range(4):
+        u = u + mm(hh[quad + s, 1], blocks(b6, s))
+    for k in range(1, 4):
+        got["u5"][k - 1].wait_recv()
+        u = u - mm(u5g[flip(zq, k)], blocks(n6, flip(zq, k)))
+    own = u.astype(bf16)
+    u6g[z] = own
+    along("u6", 8, u6g, z)
+
+    twin("x3", "t3", c3)
+    twin("x4", "t4", c4)
+    arrive("t3")
+    for s in range(8):
+        b7[16 * s : 16 * s + 16] = square(c3[:, :, s // 2, s % 2]).reshape(16, 16, 256)
+    lax.fori_loop(0, 128, move(6, 0, b7, n7), 0, unroll=8)
+    for k in range(3, 7):
+        got["h"][k].wait_recv()
+    u = -mm(own, blocks(n7, z))
+    for s in range(8):
+        u = u + mm(hh[s, 0], blocks(b7, s))
+
+    arrive("t4")
+    v5 = rs_[64:80]
+    for s in range(2):
+        i5[s] = square(c4[:, :, 1, :, 128 * s : 128 * s + 128])
+        v5 = v5 - mm_nt(u4g[s], route(4, pair + s, zp))
+    v5 = v5.astype(bf16)
+    v6 = rs_[80:96]
+    for s in range(4):
+        i6[s] = square(c4[:, :, 2 + s // 2, :, 128 * (s % 2) : 128 * (s % 2) + 128])
+        v6 = v6 - mm_nt(u5g[s], route(5, quad + s, zq))
+    v6 = v6.astype(bf16)
+    w6 = [mm(v6, i6[s]).astype(bf16) for s in range(4)]
+    for s in range(4):
+        total = mm(w6[0], route(5, quad + s, 0))
+        for t in range(1, 4):
+            total = total + mm(w6[t], route(5, quad + s, t))
+        wq6[s] = total * sign_lane
+
+    for k in range(1, 8):
+        got["u6"][k - 1].wait_recv()
+        u = u - mm(u6g[flip(z, k)], blocks(n7, flip(z, k)))
+    own = (u * sign_lane).astype(bf16)
+
+    for k in range(1, 4):
+        t = flip(zq, k)
+        d6s[k - 1] = (wq6[t] - mm_nt(own, blocks(n6, t))).astype(bf16)
+        send("d6", d6s.at[k - 1], d6r.at[k - 1], dev(flip(z, k), y, c, x))
+    below = wq6[zq] - mm_nt(own, blocks(n6, zq))
+    g6g[z] = own
+    along("g6", 8, g6g, z)
+
+    w5 = [mm(v5, i5[s]).astype(bf16) for s in range(2)]
+    for s in range(2):
+        wq5[s] = sign_lane * (
+            mm(w5[0], route(4, pair + s, 0)) + mm(w5[1], route(4, pair + s, 1))
+        )
+    rawi = c4[:, :, 0, :, 0:128].reshape(256, 128)
     for level in range(1, 4):
         i14[level - 1] = mm(small(rawi, level), natural).astype(bf16)
-    i14[3] = square(c0[:, :, :, 384:512])
+    i14[3] = square(c4[:, :, 0, :, 128:256])
     for level in range(1, 5):
         xo[16 * level - 16 : 16 * level] = mm(vs[level - 1], i14[level - 1]) * sign_lane
 
+    arrive("d6")
+    for k in range(3):
+        below = below + d6r[k].astype(f32)
+    own = below.astype(bf16)
+    below = [wq5[s] - mm_nt(own, blocks(n5, s)) for s in range(2)]
+    for s in range(2):
+        d5s[s] = below[s].astype(bf16)
+    send("d5", d5s, d5r, dev(flip(z, 1), y, c, x))
+    g5g[zq] = own
+    along("g5", 4, g5g, zq)
+
+    def emit(level, size, first, ref):
+        want = (16 * (leaf - 16 * first) + iota((16, 256), 0)).astype(f32)
+        block = jnp.zeros((16, 16), f32)
+        for s in range(size):
+            block = block + mm_nt(hot(want == dl_[first + s][level - 1 : level]), ref[s])
+        sep_out[0, level - 1] = block[0:8]
+        sep_out[1, level - 1] = -block[8:16]
+
+    arrive("g6")
+    emit(7, 8, 0, g6g)
     arrive("d5")
-    own = (below + d5r[...].astype(f32)).astype(bf16)
-    g4g[zp] = own
-    along("g4", 2, g4g, zp)
+    for s in range(2):
+        g4g[s] = (below[s] + d5r[s].astype(f32)).astype(bf16)
+    own = g4g[zp]
     now = xo[48:64] - mm_nt(own, b4[...])
     xo[48:64] = now
     for level in range(3, 0, -1):
@@ -396,16 +426,9 @@
     for level in range(4):
         sep_out[0, level] = turned[0:8, 16 * level : 16 * level + 16]
         sep_out[1, level] = -turned[8:16, 16 * level : 16 * level + 16]
-    arrive("g6")
     arrive("g5")
-    arrive("g4")
-    for level, size, first, ref in ((7, 8, 0, g6g), (6, 4, quad, g5g), (5, 2, pair, g4g)):
-        want = (16 * (leaf - 16 * first) + iota((16, 256), 0)).astype(f32)
-        block = jnp.zeros((16, 16), f32)
-        for s in range(size):
-            block = block + mm_nt(hot(want == dl_[first + s][level - 1 : level]), ref[s])
-        sep_out[0, level - 1] = block[0:8]
-        sep_out[1, level - 1] = -block[8:16]
+    emit(6, 4, quad, g5g)
+    emit(5, 2, pair, g4g)
 
     for one in pending:
         one.wait_send()
@@ -436,16 +459,17 @@
             V((2, 8, 512), bf16), V((2, 8, 2032), bf16), V((2, 8, 1008), bf16),
             V((7, 128), jnp.int32), pltpu.SemaphoreType.DMA((7,)),
             V((16, 128), f32), V((16, 3072), f32), V((8, 2, 16, 128), bf16),
-            V((8, 2, 16, 512), bf16), V((8, 2, 16, 768), bf16),
-            V((2, 16, 128), bf16), V((4, 16, 128), bf16), V((8, 16, 128), bf16),
-            V((8, 2, 2, 16, 128), bf16), V((8, 2, 4, 16, 128), bf16), V((8, 2, 8, 16, 128), bf16),
+            V((8, 2, 16, 256), bf16), V((8, 2, 4, 16, 256), bf16),
+            V((2, 16, 128), bf16), V((4, 16, 128), bf16), V((8, 16, 128), bf16), rows(4),
+            V((4, 16, 128), bf16), V((4, 2, 16, 128), bf16),
+            V((8, 2, 2, 16, 128), bf16), V((8, 2, 4, 16, 128), bf16), V((8, 2, 4, 2, 16, 128), bf16),
             V((4, 2, 16, 128), bf16), V((4, 2, 16, 128), bf16), V((16, 1024), bf16),
             V((8, 8, 256), f32), V((256, 256), bf16), squares(3),
             V((128, 256), f32), rows(4),
             squares(3), V((256, 256), bf16), rows(32), rows(64), rows(128),
             rows(32), rows(64), rows(128), squares(4), squares(2), squares(4),
-            rows(2), rows(4), rows(8), rows(2), rows(4), rows(8),
-            V((4, 16, 256), f32), V((2, 16, 256), f32), rows(3), rows(3), rows(), rows(),
+            rows(8, 3), rows(2), rows(4), rows(8),
+            V((4, 16, 256), f32), V((2, 16, 256), f32), rows(3), rows(3), rows(2), rows(2),
             rows(8), rows(4), rows(2),
             V((4, 2, 16, 512), bf16), V((3, 2, 16, 512), bf16), V((4, 2, 16, 512), f32),
             V((64, 256), f32), V((256, 64), f32),

time: 56.7 us -> 56.5 us (level)
  no operation moved by 1% of the time
where the time goes in v3:
time: 56.5 us; the launch traced here: 56.3 us
  Pallas kernels  52.9 us (94%)
  local copies, waits for them, and re-layouts  2.12 us (4%)
  between operations  1.3 us (2%)
    pallas_call x1, Pallas kernels, body(): pl.pallas_call(kernel, out_shape=(jax.ShapeDtypeStruct((2, 16, 512), f32)...  52.9 us
    unnamed x4, local copies, waits for them, and re-layouts  2.12 us

profile of v3, /device:TPU:1, one launch (start us, length us, event | category | flops | bytes accessed | tf_op | source)
XLA Modules:
  0.0 56.3 jit_solution(10826422356438909927)
XLA Ops:
  1.3 52.9 %shard_map.95 = (f32[2,16,512]{2,1,0:T(8,128)}, f32[2,7,8,16]{3,2,1,0:T(8,128)}) custom-call(f32[2,16,512]{2,1,0:T(8,128)} %rhs_hbm.1, f32[2,7,8,16]{3,2,1,0:T(8,128)} %bitcast.3, bf16[2,128,512]{2,1,0:T(8,128)(2,1)} %inv_hbm.1, bf16[2,8,512]{2,1,0:T(8,128)(2,1)} %bitcast.5, bf16[2,8,2032]{2,1,0:T(8,128)(2,1)} %sinv_hbm.1, bf16[2,8,1008]{2,1,0:T(8,128)(2,1)} %slow_hbm.1, ...), custom_call_target="tpu_custom_call" | custom-call | tf_op jit(solution)/shard_map/pallas_call | solution.py:449
  54.2 0.0 copy-start
  54.2 1.5 %copy.13 = f32[2,16,512]{2,1,0:T(8,128)} copy(f32[2,16,512]{2,1,0:T(8,128)} %get-tuple-element.8) | data formatting | bytes 131072
  55.7 0.0 copy-done
  55.7 0.6 %copy.14 = f32[2,16,7,8]{1,3,2,0:T(8,128)} copy(f32[2,16,7,8]{1,3,2,0:T(8,128)S(1)} %bitcast.4) | data formatting | bytes 14336
Async XLA Ops:
  54.2 1.5 %copy-start = (f32[2,7,8,16]{3,2,1,0:T(8,128)S(1)}, f32[2,7,8,16]{3,2,1,0:T(8,128)}, u32[]{:S(2)}) copy-start(f32[2,7,8,16]{3,2,1,0:T(8,128)} %get-tuple-element.5) | copy-start | bytes 21508

commit v4 on v3

--- a/solution.py
+++ b/solution.py
@@ -11,7 +11,7 @@
 
 COUNTS = dict(
     msg=15, zx=3, c0=7, c4=7, q1=1, q2=3, q3=7, c1=7, c2=7, c3=7, t0=1, t1=1, t2=1, t3=1, t4=1,
-    x2=3, x3=3, x4=3, h=7, u4=1, u5=3, u6=7, d6=3, d5=1, g6=7, g5=3, lw=3,
+    x2=3, x3=3, x4=3, h=7, u4=1, u5=3, u6=7, d6=3, d5=1, g6=7, e6=3, lw=3,
 )
 FIRST = {}
 _total = 0
@@ -47,17 +47,17 @@
 
 
 def kernel(
-    rhs_hbm, sep_hbm, inv_hbm, low_hbm, sinv_hbm, slow_hbm, tgt_hbm, live_ref, tgs,
+    rhs_hbm, sep_hbm, inv_hbm, low_hbm, sinv_hbm, slow_hbm, tgt_hbm, live_ref,
     leaf_out, sep_out,
-    rhs_ref, sep_ref, inv_ref, low_ref, sinv_ref, slow_ref, tgt_ref, lsem,
+    rhs_ref, sep_ref, inv_ref, low_ref, sinv_ref, slow_ref, tgt_ref, tgs, lsem,
     st, pk, m0, c0, c4, p1, p2, p3, p4, z2, z3, c1, c2, c3, zxs, zxr, eh, dl_, p0, pis, rs_, vs,
     m123, b4, b5, b6, b7, n5, n6, n7, i14, i5, i6, hh, u4g, u5g, u6g,
-    wq6, wq5, d6s, d6r, d5s, d5r, g6g, g5g, g4g, lws, lwr, lwo, xo, xt, ssem, rsem,
+    wq6, wq5, wn6, e6s, e6r, d6s, d6r, d5s, d5r, g6g, g4g, lws, lwr, lwo, xo, xt, ssem, rsem,
 ):
     loads = []
     for j, (src, dst) in enumerate((
         (rhs_hbm, rhs_ref), (low_hbm, low_ref), (sep_hbm, sep_ref), (slow_hbm, slow_ref),
-        (sinv_hbm, sinv_ref), (tgt_hbm, tgt_ref), (inv_hbm, inv_ref),
+        (sinv_hbm, sinv_ref), (tgt_hbm, tgt_ref), (inv_hbm, inv_ref), (tgt_hbm, tgs),
     )):
         loads.append(pltpu.make_async_copy(src, dst, lsem.at[j]))
         loads[-1].start()
@@ -75,18 +75,20 @@
     def dev(zz, yy, cc, xx):
         return (zz * 16 + yy * 2 + cc, xx)
 
-    layer = [(k >> 1, k & 1) for k in range(1, 16)]
+    layer = [(ky, kc) for ky in (4, 3, 5, 2, 6, 7, 1, 0) for kc in (0, 1) if ky or kc]
     barrier = pltpu.get_barrier_semaphore()
 
     def greet(device):
         pl.semaphore_signal(barrier, inc=1, device_id=device, device_id_type=MESH)
 
-    for ky, kc in layer:
-        greet(dev(z, flip(y, ky), flip(c, kc), x))
-    for k in range(1, 8):
+    far = (4, 3, 5, 2, 6, 7, 1)
+    for k in far:
         greet(dev(flip(z, k), y, c, x))
-    for k in range(1, 4):
+        greet(dev(z, flip(y, k), c, x))
+        greet(dev(z, flip(y, k), 1 - c, x))
+    for k in (2, 1, 3):
         greet(dev(z, y, c, flip(x, k)))
+    greet(dev(z, y, 1 - c, x))
 
     pending = []
     got = {name: [] for name in COUNTS}
@@ -167,6 +169,7 @@
     c1[y, c, zp] = p1[zp]
     z2[zq] = p2[zq]
     loads[5].wait()
+    loads[7].wait()
     tgt = tgt_ref[...].astype(f32).astype(bf16)
     spot = iota((128, 1024), 1)
     wide = mm(tgt, hot(iota((128, 1024), 0) == spot // 8))
@@ -181,15 +184,14 @@
 
     pl.semaphore_wait(barrier, 25)
 
+    scatter("c0", c0)
     for ky, kc in layer:
         send("msg", m0.at[y, c], m0.at[y, c], dev(z, flip(y, ky), flip(c, kc), x))
-    scatter("c0", c0)
     send("q1", p1.at[1 - zp], c1.at[y, c, zp], dev(flip(z, 1), y, c, x))
     for k in range(1, 4):
         send("q2", p2.at[flip(zq, k)], z2.at[zq], dev(flip(z, k), y, c, x))
     for k in range(1, 8):
         send("q3", p3.at[flip(z, k)], z3.at[lax.div(z, 2), zp], dev(flip(z, k), y, c, x))
-    quarter("c4", c4)
     for k in range(1, 4):
         send("zx", zxs.at[flip(x, k)], zxr.at[x], dev(z, y, c, flip(x, k)))
 
@@ -236,18 +238,21 @@
     def blocks(ref, s):
         return ref[pl.ds(16 * s, 16)].reshape(256, 256)
 
+    arrive("q1")
+    scatter("c1", c1)
+    twin("c0", "t0", c0)
+    arrive("q2")
+    c2[y, c, x] = z2[x]
+    quarter("c2", c2)
+    arrive("q3")
+    c3[y, c, x] = z3[x]
+    quarter("c3", c3)
     arrive("msg")
     flipped = jnp.transpose(m0[...].reshape(256, 128).astype(f32))
     rs_[...] = flipped
     u = mm_nt(flipped[112:128].astype(bf16), p0[...])
     v = (flipped[0:16] - u).astype(bf16)
     vs[0] = v
-    twin("c0", "t0", c0)
-    arrive("q1")
-    scatter("c1", c1)
-    arrive("q2")
-    c2[y, c, x] = z2[x]
-    quarter("c2", c2)
     arrive("t0")
     raw0 = c0[:, :, :, 0:128].reshape(256, 128)
     for level in range(1, 4):
@@ -265,11 +270,33 @@
     for k in range(1, 8):
         part = pl.ds(0, 3 if k < 2 else 2 if k < 4 else 1)
         send("h", hh.at[z, part], hh.at[z, part], dev(flip(z, k), y, c, x))
-    arrive("q3")
-    c3[y, c, x] = z3[x]
-    quarter("c3", c3)
+    quarter("c4", c4)
 
     twin("c1", "t1", c1)
+    planes("c2", "x2", c2)
+    arrive("t1")
+    for s in range(2):
+        b5[16 * s : 16 * s + 16] = square(c1[:, :, s]).reshape(16, 16, 256)
+
+    def move(level, first, source, target):
+        def step(i, carry):
+            target[i] = source[tgs[level, first + i]]
+            return carry
+        return step
+
+    lax.fori_loop(0, 32, move(4, 16 * pair, b5, n5), 0, unroll=8)
+    got["h"][0].wait_recv()
+    u = -mm(own, blocks(n5, zp))
+    for s in range(2):
+        u = u + mm(hh[pair + s, 2], blocks(b5, s))
+    arrive("u4")
+    u = u - mm(u4g[1 - zp], blocks(n5, 1 - zp))
+    own = u.astype(bf16)
+    u5g[zq] = own
+    along("u5", 4, u5g, zq)
+
+    planes("c3", "x3", c3)
+    twin("x2", "t2", c2)
     planes("c4", "x4", c4)
     arrive("zx")
     loads[6].wait()
@@ -284,30 +311,6 @@
     lws[:, 1] = imag.astype(bf16)
     for k in range(1, 4):
         send("lw", lws.at[flip(x, k)], lwr.at[k - 1], dev(z, y, c, flip(x, k)))
-    planes("c2", "x2", c2)
-    arrive("t1")
-    for s in range(2):
-        b5[16 * s : 16 * s + 16] = square(c1[:, :, s]).reshape(16, 16, 256)
-
-    def move(level, first, source, target):
-        def step(i, carry):
-            target[i] = source[tgs[level, first + i]]
-            return carry
-        return step
-
-    lax.fori_loop(0, 32, move(4, 16 * pair, b5, n5), 0, unroll=8)
-    got["h"][0].wait_recv()
-    u = -mm(own, blocks(n5, zp))
-    for s in range(2):
-        u = u + mm(hh[pair + s, 2], blocks(b5, s))
-    arrive("u4")
-    u = u - mm(u4g[1 - zp], blocks(n5, 1 - zp))
-    own = u.astype(bf16)
-    u5g[zq] = own
-    along("u5", 4, u5g, zq)
-
-    twin("x2", "t2", c2)
-    planes("c3", "x3", c3)
     arrive("t2")
     for s in range(4):
         b6[16 * s : 16 * s + 16] = square(c2[:, :, s]).reshape(16, 16, 256)
@@ -347,7 +350,11 @@
         i6[s] = square(c4[:, :, 2 + s // 2, :, 128 * (s % 2) : 128 * (s % 2) + 128])
         v6 = v6 - mm_nt(u5g[s], route(5, quad + s, zq))
     v6 = v6.astype(bf16)
-    w6 = [mm(v6, i6[s]).astype(bf16) for s in range(4)]
+    w6 = []
+    for s in range(4):
+        part = mm(v6, i6[s])
+        wn6[s] = part * sign_lane
+        w6.append(part.astype(bf16))
     for s in range(4):
         total = mm(w6[0], route(5, quad + s, 0))
         for t in range(1, 4):
@@ -366,6 +373,11 @@
     below = wq6[zq] - mm_nt(own, blocks(n6, zq))
     g6g[z] = own
     along("g6", 8, g6g, z)
+    for k in range(1, 4):
+        t = flip(zq, k)
+        e6s[k - 1] = (wn6[t] - mm_nt(own, blocks(b6, t))).astype(bf16)
+        send("e6", e6s.at[k - 1], e6r.at[k - 1], dev(flip(z, k), y, c, x))
+    sixth = wn6[zq] - mm_nt(own, blocks(b6, zq))
 
     w5 = [mm(v5, i5[s]).astype(bf16) for s in range(2)]
     for s in range(2):
@@ -387,8 +399,6 @@
     for s in range(2):
         d5s[s] = below[s].astype(bf16)
     send("d5", d5s, d5r, dev(flip(z, 1), y, c, x))
-    g5g[zq] = own
-    along("g5", 4, g5g, zq)
 
     def emit(level, size, first, ref):
         want = (16 * (leaf - 16 * first) + iota((16, 256), 0)).astype(f32)
@@ -420,14 +430,17 @@
     leaf_out[0] = jnp.where(mask, mine[0] - less[:, 0:512], 0.0)
     leaf_out[1] = jnp.where(mask, mine[1] + less[:, 512:1024], 0.0)
 
+    arrive("e6")
+    for k in range(3):
+        sixth = sixth + e6r[k].astype(f32)
+    xo[64:80] = sixth
+    xo[80:128] = jnp.zeros((48, 256), f32)
     xt[...] = jnp.transpose(xo[...])
     start = pl.multiple_of(dl * 16, 16)
     turned = xt[pl.ds(start, 16), :]
-    for level in range(4):
-        sep_out[0, level] = turned[0:8, 16 * level : 16 * level + 16]
-        sep_out[1, level] = -turned[8:16, 16 * level : 16 * level + 16]
-    arrive("g5")
-    emit(6, 4, quad, g5g)
+    for row, level in enumerate((0, 1, 2, 3, 5)):
+        sep_out[0, level] = turned[0:8, 16 * row : 16 * row + 16]
+        sep_out[1, level] = -turned[8:16, 16 * row : 16 * row + 16]
     emit(5, 2, pair, g4g)
 
     for one in pending:
@@ -452,12 +465,13 @@
             jax.ShapeDtypeStruct((2, 16, 512), f32),
             jax.ShapeDtypeStruct((2, 7, 8, 16), f32),
         ),
-        in_specs=[hb, hb, hb, hb, hb, hb, hb, sm, sm],
+        in_specs=[hb] * 7 + [sm],
         out_specs=(vm, vm),
         scratch_shapes=[
             V((2, 16, 512), f32), V((2, 7, 8, 16), f32), V((2, 128, 512), bf16),
             V((2, 8, 512), bf16), V((2, 8, 2032), bf16), V((2, 8, 1008), bf16),
-            V((7, 128), jnp.int32), pltpu.SemaphoreType.DMA((7,)),
+            V((7, 128), jnp.int32), pltpu.SMEM((7, 128), jnp.int32),
+            pltpu.SemaphoreType.DMA((8,)),
             V((16, 128), f32), V((16, 3072), f32), V((8, 2, 16, 128), bf16),
             V((8, 2, 16, 256), bf16), V((8, 2, 4, 16, 256), bf16),
             V((2, 16, 128), bf16), V((4, 16, 128), bf16), V((8, 16, 128), bf16), rows(4),
@@ -469,18 +483,21 @@
             squares(3), V((256, 256), bf16), rows(32), rows(64), rows(128),
             rows(32), rows(64), rows(128), squares(4), squares(2), squares(4),
             rows(8, 3), rows(2), rows(4), rows(8),
-            V((4, 16, 256), f32), V((2, 16, 256), f32), rows(3), rows(3), rows(2), rows(2),
-            rows(8), rows(4), rows(2),
+            V((4, 16, 256), f32), V((2, 16, 256), f32), V((4, 16, 256), f32), rows(3), rows(3), rows(3), rows(3), rows(2), rows(2),
+            rows(8), rows(2),
             V((4, 2, 16, 512), bf16), V((3, 2, 16, 512), bf16), V((4, 2, 16, 512), f32),
-            V((64, 256), f32), V((256, 64), f32),
+            V((128, 256), f32), V((256, 128), f32),
             pltpu.SemaphoreType.DMA((COPIES,)), pltpu.SemaphoreType.DMA((COPIES,)),
         ],
         compiler_params=pltpu.CompilerParams(
-            collective_id=0, has_side_effects=True, vmem_limit_bytes=60 * 2**20
+            collective_id=0, has_side_effects=True, vmem_limit_bytes=40 * 2**20
         ),
     )(
-        leaf_rhs, sep_rhs.transpose(0, 2, 3, 1), leaf_inv, leaf_low.transpose(0, 2, 1),
-        sep_inv, sep_low, targets, leaf_live, targets,
+        *(pltpu.with_memory_space_constraint(one, pltpu.HBM) for one in (
+            leaf_rhs, sep_rhs.transpose(0, 2, 3, 1), leaf_inv, leaf_low.transpose(0, 2, 1),
+            sep_inv, sep_low, targets,
+        )),
+        leaf_live,
     )
     return out_leaf, out_sep.transpose(0, 3, 1, 2)
 

time: 56.5 us -> 51.7 us (0.915)
  Pallas kernels: 52.9 us -> 49 us
  local copies, waits for them, and re-layouts: 2.12 us -> 1.25 us
    pallas_call x1, Pallas kernels: 52.9 us -> 49 us  [body(): pl.pallas_call(kernel, out_shape=(jax.ShapeDtypeStruct((2, 16, 512), f32)...]
    unnamed x4 -> x2, local copies, waits for them, and re-layouts: 2.12 us -> 1.25 us
where the time goes in v4:
time: 51.7 us; the launch traced here: 51.6 us
  Pallas kernels  49 us (95%)
  between operations  1.29 us (2%)
  local copies, waits for them, and re-layouts  1.25 us (2%)
    pallas_call x1, Pallas kernels, body(): pl.pallas_call(kernel, out_shape=(jax.ShapeDtypeStruct((2, 16, 512), f32)...  49 us
    unnamed x2, local copies, waits for them, and re-layouts  1.25 us

profile of v4, /device:TPU:1, one launch (start us, length us, event | category | flops | bytes accessed | tf_op | source)
XLA Modules:
  0.0 51.6 jit_solution(9960717591340918314)
XLA Ops:
  1.3 49.0 %shard_map.95 = (f32[2,16,512]{2,1,0:T(8,128)S(1)}, f32[2,7,8,16]{3,2,1,0:T(8,128)S(1)}) custom-call(f32[2,16,512]{2,1,0:T(8,128)} %rhs_hbm.1, f32[2,7,8,16]{3,2,1,0:T(8,128)} %bitcast.4, bf16[2,128,512]{2,1,0:T(8,128)(2,1)} %inv_hbm.1, bf16[2,8,512]{2,1,0:T(8,128)(2,1)} %bitcast.5, bf16[2,8,2032]{2,1,0:T(8,128)(2,1)} %sinv_hbm.1, ...), custom_call_target="tpu_custom_call" | custom-call | tf_op jit(solution)/shard_map/pallas_call | solution.py:462
  50.3 0.6 %copy.13 = f32[2,16,512]{2,1,0:T(8,128)} copy(f32[2,16,512]{2,1,0:T(8,128)S(1)} %get-tuple-element.8) | data formatting | bytes 131072
  50.9 0.6 %copy.14 = f32[2,16,7,8]{1,3,2,0:T(8,128)} copy(f32[2,16,7,8]{1,3,2,0:T(8,128)S(1)} %bitcast.3) | data formatting | bytes 14336

commit v5 on v4

--- a/solution.py
+++ b/solution.py
@@ -10,8 +10,8 @@
 f32 = jnp.float32
 
 COUNTS = dict(
-    msg=15, zx=3, c0=7, c4=7, q1=1, q2=3, q3=7, c1=7, c2=7, c3=7, t0=1, t1=1, t2=1, t3=1, t4=1,
-    x2=3, x3=3, x4=3, h=7, u4=1, u5=3, u6=7, d6=3, d5=1, g6=7, e6=3, lw=3,
+    msg=15, zx=3, c0=7, c4=7, c5=7, q0=1, q1=1, q2=3, q3=7, c1=7, c2=7, c3=7, t0=1, t1=1, t2=1, t3=1, t4=1, t5=1,
+    x2=3, x3=3, x4=3, h=7, u4=1, u5=3, u6=7, d6=3, f5=1, g6=7, e6=3, lw=3,
 )
 FIRST = {}
 _total = 0
@@ -50,9 +50,9 @@
     rhs_hbm, sep_hbm, inv_hbm, low_hbm, sinv_hbm, slow_hbm, tgt_hbm, live_ref,
     leaf_out, sep_out,
     rhs_ref, sep_ref, inv_ref, low_ref, sinv_ref, slow_ref, tgt_ref, tgs, lsem,
-    st, pk, m0, c0, c4, p1, p2, p3, p4, z2, z3, c1, c2, c3, zxs, zxr, eh, dl_, p0, pis, rs_, vs,
-    m123, b4, b5, b6, b7, n5, n6, n7, i14, i5, i6, hh, u4g, u5g, u6g,
-    wq6, wq5, wn6, e6s, e6r, d6s, d6r, d5s, d5r, g6g, g4g, lws, lwr, lwo, xo, xt, ssem, rsem,
+    st, pk, m0, c0, c4, p1, p2, p3, p4, z2, z3, c1, c2, c3, c5, zxs, zxr, eh, dl_, p0, pis, rs_, vs,
+    m123, b4, b5, b6, b7, b5o, n5o, n5, n6, n7, i14, i5, i6, hh, u4g, u5g, u6g,
+    wq6, wq5, wn6, wn5, e6s, e6r, d6s, d6r, f5s, f5r, g6g, g5v, lws, lwr, lwo, xo, xt, ssem, rsem,
 ):
     loads = []
     for j, (src, dst) in enumerate((
@@ -92,9 +92,10 @@
 
     pending = []
     got = {name: [] for name in COUNTS}
-
-    def send(name, src, dst, device):
-        index = FIRST[name] + len(got[name])
+    by = {}
+
+    def send(name, src, dst, device, at=None):
+        index = FIRST[name] + (len(got[name]) if at is None else at)
         out = pltpu.make_async_remote_copy(
             src_ref=src, dst_ref=dst, send_sem=ssem.at[index], recv_sem=rsem.at[index],
             device_id=device, device_id_type=MESH,
@@ -102,6 +103,7 @@
         out.start()
         pending.append(out)
         got[name].append(out)
+        by[name, index - FIRST[name]] = out
 
     def arrive(name):
         for one in got[name]:
@@ -125,8 +127,9 @@
         send(tag, buf.at[:, c], buf.at[:, c], dev(z, y, 1 - c, x))
 
     def along(name, count, buf, slot):
-        for k in range(1, count):
-            send(name, buf.at[slot], buf.at[slot], dev(flip(z, k), y, c, x))
+        for k in far:
+            if k < count:
+                send(name, buf.at[slot], buf.at[slot], dev(flip(z, k), y, c, x), k - 1)
 
     loads[0].wait()
     loads[1].wait()
@@ -167,6 +170,7 @@
     for t in range(4):
         p2[t] = pk[:, 512 + 128 * t : 640 + 128 * t].astype(bf16)
     c1[y, c, zp] = p1[zp]
+    c5[y, c, zp] = p1[1 - zp]
     z2[zq] = p2[zq]
     loads[5].wait()
     loads[7].wait()
@@ -192,6 +196,8 @@
         send("q2", p2.at[flip(zq, k)], z2.at[zq], dev(flip(z, k), y, c, x))
     for k in range(1, 8):
         send("q3", p3.at[flip(z, k)], z3.at[lax.div(z, 2), zp], dev(flip(z, k), y, c, x))
+    quarter("c4", c4)
+    send("q0", p1.at[zp], c5.at[y, c, zp], dev(flip(z, 1), y, c, x))
     for k in range(1, 4):
         send("zx", zxs.at[flip(x, k)], zxr.at[x], dev(z, y, c, flip(x, k)))
 
@@ -270,10 +276,12 @@
     for k in range(1, 8):
         part = pl.ds(0, 3 if k < 2 else 2 if k < 4 else 1)
         send("h", hh.at[z, part], hh.at[z, part], dev(flip(z, k), y, c, x))
-    quarter("c4", c4)
+    planes("c4", "x4", c4)
 
     twin("c1", "t1", c1)
     planes("c2", "x2", c2)
+    arrive("q0")
+    scatter("c5", c5)
     arrive("t1")
     for s in range(2):
         b5[16 * s : 16 * s + 16] = square(c1[:, :, s]).reshape(16, 16, 256)
@@ -296,8 +304,6 @@
     along("u5", 4, u5g, zq)
 
     planes("c3", "x3", c3)
-    twin("x2", "t2", c2)
-    planes("c4", "x4", c4)
     arrive("zx")
     loads[6].wait()
     zr4 = zxr[:, 0].reshape(64, 128)
@@ -311,6 +317,8 @@
     lws[:, 1] = imag.astype(bf16)
     for k in range(1, 4):
         send("lw", lws.at[flip(x, k)], lwr.at[k - 1], dev(z, y, c, flip(x, k)))
+    twin("x2", "t2", c2)
+    twin("x4", "t4", c4)
     arrive("t2")
     for s in range(4):
         b6[16 * s : 16 * s + 16] = square(c2[:, :, s]).reshape(16, 16, 256)
@@ -320,15 +328,14 @@
     u = -mm(own, blocks(n6, zq))
     for s in range(4):
         u = u + mm(hh[quad + s, 1], blocks(b6, s))
-    for k in range(1, 4):
-        got["u5"][k - 1].wait_recv()
+    for k in (1, 2, 3):
+        by["u5", k - 1].wait_recv()
         u = u - mm(u5g[flip(zq, k)], blocks(n6, flip(zq, k)))
     own = u.astype(bf16)
     u6g[z] = own
     along("u6", 8, u6g, z)
 
     twin("x3", "t3", c3)
-    twin("x4", "t4", c4)
     arrive("t3")
     for s in range(8):
         b7[16 * s : 16 * s + 16] = square(c3[:, :, s // 2, s % 2]).reshape(16, 16, 256)
@@ -339,12 +346,25 @@
     for s in range(8):
         u = u + mm(hh[s, 0], blocks(b7, s))
 
+    twin("c5", "t5", c5)
     arrive("t4")
     v5 = rs_[64:80]
     for s in range(2):
         i5[s] = square(c4[:, :, 1, :, 128 * s : 128 * s + 128])
         v5 = v5 - mm_nt(u4g[s], route(4, pair + s, zp))
     v5 = v5.astype(bf16)
+    w5 = []
+    for s in range(2):
+        part = mm(v5, i5[s])
+        wn5[s] = part * sign_lane
+        w5.append(part.astype(bf16))
+    for s in range(2):
+        wq5[s] = sign_lane * (
+            mm(w5[0], route(4, pair + s, 0)) + mm(w5[1], route(4, pair + s, 1))
+        )
+    f5s[0] = wq5[1 - zp].astype(bf16)
+    f5s[1] = wn5[1 - zp].astype(bf16)
+    send("f5", f5s, f5r, dev(flip(z, 1), y, c, x))
     v6 = rs_[80:96]
     for s in range(4):
         i6[s] = square(c4[:, :, 2 + s // 2, :, 128 * (s % 2) : 128 * (s % 2) + 128])
@@ -361,29 +381,30 @@
             total = total + mm(w6[t], route(5, quad + s, t))
         wq6[s] = total * sign_lane
 
-    for k in range(1, 8):
-        got["u6"][k - 1].wait_recv()
+    for k in (1, 7, 2, 6, 3, 5, 4):
+        by["u6", k - 1].wait_recv()
         u = u - mm(u6g[flip(z, k)], blocks(n7, flip(z, k)))
     own = (u * sign_lane).astype(bf16)
 
-    for k in range(1, 4):
-        t = flip(zq, k)
-        d6s[k - 1] = (wq6[t] - mm_nt(own, blocks(n6, t))).astype(bf16)
-        send("d6", d6s.at[k - 1], d6r.at[k - 1], dev(flip(z, k), y, c, x))
-    below = wq6[zq] - mm_nt(own, blocks(n6, zq))
     g6g[z] = own
-    along("g6", 8, g6g, z)
+    for k in far[:3]:
+        send("g6", g6g.at[z], g6g.at[z], dev(flip(z, k), y, c, x), k - 1)
+    half = zq - zp
+    for first, targets_k in ((2 - half, (2, 3)), (half, (1,))):
+        for j in range(2):
+            part = wq6[first + j] - mm_nt(own, blocks(n6, first + j))
+            wq6[first + j] = part
+            d6s[first + j] = part.astype(bf16)
+        for k in targets_k:
+            send("d6", d6s.at[pl.ds(first, 2)], d6r.at[k - 1], dev(flip(z, k), y, c, x), k - 1)
+    for k in far[3:]:
+        send("g6", g6g.at[z], g6g.at[z], dev(flip(z, k), y, c, x), k - 1)
     for k in range(1, 4):
         t = flip(zq, k)
         e6s[k - 1] = (wn6[t] - mm_nt(own, blocks(b6, t))).astype(bf16)
         send("e6", e6s.at[k - 1], e6r.at[k - 1], dev(flip(z, k), y, c, x))
     sixth = wn6[zq] - mm_nt(own, blocks(b6, zq))
 
-    w5 = [mm(v5, i5[s]).astype(bf16) for s in range(2)]
-    for s in range(2):
-        wq5[s] = sign_lane * (
-            mm(w5[0], route(4, pair + s, 0)) + mm(w5[1], route(4, pair + s, 1))
-        )
     rawi = c4[:, :, 0, :, 0:128].reshape(256, 128)
     for level in range(1, 4):
         i14[level - 1] = mm(small(rawi, level), natural).astype(bf16)
@@ -391,14 +412,18 @@
     for level in range(1, 5):
         xo[16 * level - 16 : 16 * level] = mm(vs[level - 1], i14[level - 1]) * sign_lane
 
+    arrive("t5")
+    for s in range(2):
+        b5o[16 * s : 16 * s + 16] = square(c5[:, :, s]).reshape(16, 16, 256)
+    lax.fori_loop(0, 32, move(4, 16 * pair, b5o, n5o), 0, unroll=8)
+    arrive("f5")
+    parent = wq5[zp] + f5r[0].astype(f32)
     arrive("d6")
-    for k in range(3):
-        below = below + d6r[k].astype(f32)
-    own = below.astype(bf16)
-    below = [wq5[s] - mm_nt(own, blocks(n5, s)) for s in range(2)]
-    for s in range(2):
-        d5s[s] = below[s].astype(bf16)
-    send("d5", d5s, d5r, dev(flip(z, 1), y, c, x))
+    for j in range(2):
+        below = wq6[half + j]
+        for k in range(3):
+            below = below + d6r[k, j].astype(f32)
+        g5v[j] = below.astype(bf16)
 
     def emit(level, size, first, ref):
         want = (16 * (leaf - 16 * first) + iota((16, 256), 0)).astype(f32)
@@ -408,19 +433,15 @@
         sep_out[0, level - 1] = block[0:8]
         sep_out[1, level - 1] = -block[8:16]
 
-    arrive("g6")
-    emit(7, 8, 0, g6g)
-    arrive("d5")
-    for s in range(2):
-        g4g[s] = (below[s] + d5r[s].astype(f32)).astype(bf16)
-    own = g4g[zp]
+    own = parent - mm_nt(g5v[zp], blocks(n5, zp)) - mm_nt(g5v[1 - zp], blocks(n5o, zp))
+    own = own.astype(bf16)
     now = xo[48:64] - mm_nt(own, b4[...])
     xo[48:64] = now
     for level in range(3, 0, -1):
         now = xo[16 * level - 16 : 16 * level] - mm_nt(now.astype(bf16), m123[level - 1])
         xo[16 * level - 16 : 16 * level] = now
-    parent = 16 * (dl - c + tgs[0, leaf])
-    chosen = hot(iota((16, 256), 1) == parent + iota((16, 256), 0))
+    above = 16 * (dl - c + tgs[0, leaf])
+    chosen = hot(iota((16, 256), 1) == above + iota((16, 256), 0))
     back = mm_nt(now.astype(bf16), chosen).astype(bf16)
     less = mm(back, eh[...])
     arrive("lw")
@@ -434,14 +455,19 @@
     for k in range(3):
         sixth = sixth + e6r[k].astype(f32)
     xo[64:80] = sixth
-    xo[80:128] = jnp.zeros((48, 256), f32)
+    xo[80:96] = (
+        wn5[zp] + f5r[1].astype(f32)
+        - mm_nt(g5v[zp], blocks(b5, zp)) - mm_nt(g5v[1 - zp], blocks(b5o, zp))
+    )
+    xo[96:128] = jnp.zeros((32, 256), f32)
     xt[...] = jnp.transpose(xo[...])
     start = pl.multiple_of(dl * 16, 16)
     turned = xt[pl.ds(start, 16), :]
-    for row, level in enumerate((0, 1, 2, 3, 5)):
+    for row, level in enumerate((0, 1, 2, 3, 5, 4)):
         sep_out[0, level] = turned[0:8, 16 * row : 16 * row + 16]
         sep_out[1, level] = -turned[8:16, 16 * row : 16 * row + 16]
-    emit(5, 2, pair, g4g)
+    arrive("g6")
+    emit(7, 8, 0, g6g)
 
     for one in pending:
         one.wait_send()
@@ -476,14 +502,14 @@
             V((8, 2, 16, 256), bf16), V((8, 2, 4, 16, 256), bf16),
             V((2, 16, 128), bf16), V((4, 16, 128), bf16), V((8, 16, 128), bf16), rows(4),
             V((4, 16, 128), bf16), V((4, 2, 16, 128), bf16),
-            V((8, 2, 2, 16, 128), bf16), V((8, 2, 4, 16, 128), bf16), V((8, 2, 4, 2, 16, 128), bf16),
+            V((8, 2, 2, 16, 128), bf16), V((8, 2, 4, 16, 128), bf16), V((8, 2, 4, 2, 16, 128), bf16), V((8, 2, 2, 16, 128), bf16),
             V((4, 2, 16, 128), bf16), V((4, 2, 16, 128), bf16), V((16, 1024), bf16),
             V((8, 8, 256), f32), V((256, 256), bf16), squares(3),
             V((128, 256), f32), rows(4),
-            squares(3), V((256, 256), bf16), rows(32), rows(64), rows(128),
+            squares(3), V((256, 256), bf16), rows(32), rows(64), rows(128), rows(32), rows(32),
             rows(32), rows(64), rows(128), squares(4), squares(2), squares(4),
             rows(8, 3), rows(2), rows(4), rows(8),
-            V((4, 16, 256), f32), V((2, 16, 256), f32), V((4, 16, 256), f32), rows(3), rows(3), rows(3), rows(3), rows(2), rows(2),
+            V((4, 16, 256), f32), V((2, 16, 256), f32), V((4, 16, 256), f32), V((2, 16, 256), f32), rows(3), rows(3), rows(4), rows(3, 2), rows(2), rows(2),
             rows(8), rows(2),
             V((4, 2, 16, 512), bf16), V((3, 2, 16, 512), bf16), V((4, 2, 16, 512), f32),
             V((128, 256), f32), V((256, 128), f32),

time: 51.7 us -> 51.6 us (level)
  no operation moved by 1% of the time
where the time goes in v5:
time: 51.6 us; the launch traced here: 51.5 us
  Pallas kernels  48.9 us (95%)
  between operations  1.29 us (2%)
  local copies, waits for them, and re-layouts  1.25 us (2%)
    pallas_call x1, Pallas kernels, body(): pl.pallas_call(kernel, out_shape=(jax.ShapeDtypeStruct((2, 16, 512), f32)...  48.9 us
    unnamed x2, local copies, waits for them, and re-layouts  1.25 us

profile of v5, /device:TPU:1, one launch (start us, length us, event | category | flops | bytes accessed | tf_op | source)
XLA Modules:
  0.0 51.5 jit_solution(3812094003916359734)
XLA Ops:
  1.3 48.9 %shard_map.95 = (f32[2,16,512]{2,1,0:T(8,128)S(1)}, f32[2,7,8,16]{3,2,1,0:T(8,128)S(1)}) custom-call(f32[2,16,512]{2,1,0:T(8,128)} %rhs_hbm.1, f32[2,7,8,16]{3,2,1,0:T(8,128)} %bitcast.4, bf16[2,128,512]{2,1,0:T(8,128)(2,1)} %inv_hbm.1, bf16[2,8,512]{2,1,0:T(8,128)(2,1)} %bitcast.5, bf16[2,8,2032]{2,1,0:T(8,128)(2,1)} %sinv_hbm.1, ...), custom_call_target="tpu_custom_call" | custom-call | tf_op jit(solution)/shard_map/pallas_call | solution.py:488
  50.2 0.6 %copy.13 = f32[2,16,512]{2,1,0:T(8,128)} copy(f32[2,16,512]{2,1,0:T(8,128)S(1)} %get-tuple-element.8) | data formatting | bytes 131072
  50.8 0.6 %copy.14 = f32[2,16,7,8]{1,3,2,0:T(8,128)} copy(f32[2,16,7,8]{1,3,2,0:T(8,128)S(1)} %bitcast.3) | data formatting | bytes 14336

commit v6 on v5

--- a/solution.py
+++ b/solution.py
@@ -11,7 +11,7 @@
 
 COUNTS = dict(
     msg=15, zx=3, c0=7, c4=7, c5=7, q0=1, q1=1, q2=3, q3=7, c1=7, c2=7, c3=7, t0=1, t1=1, t2=1, t3=1, t4=1, t5=1,
-    x2=3, x3=3, x4=3, h=7, u4=1, u5=3, u6=7, d6=3, f5=1, g6=7, e6=3, lw=3,
+    x3=3, x4=3, h=7, u4=1, u5=3, u6=7, d6=3, f5=1, g6=7, e6=3, lw=3,
 )
 FIRST = {}
 _total = 0
@@ -188,14 +188,14 @@
 
     pl.semaphore_wait(barrier, 25)
 
+    for k in far:
+        send("q3", p3.at[flip(z, k)], z3.at[lax.div(z, 2), zp], dev(flip(z, k), y, c, x), k - 1)
     scatter("c0", c0)
     for ky, kc in layer:
         send("msg", m0.at[y, c], m0.at[y, c], dev(z, flip(y, ky), flip(c, kc), x))
     send("q1", p1.at[1 - zp], c1.at[y, c, zp], dev(flip(z, 1), y, c, x))
     for k in range(1, 4):
         send("q2", p2.at[flip(zq, k)], z2.at[zq], dev(flip(z, k), y, c, x))
-    for k in range(1, 8):
-        send("q3", p3.at[flip(z, k)], z3.at[lax.div(z, 2), zp], dev(flip(z, k), y, c, x))
     quarter("c4", c4)
     send("q0", p1.at[zp], c5.at[y, c, zp], dev(flip(z, 1), y, c, x))
     for k in range(1, 4):
@@ -244,15 +244,15 @@
     def blocks(ref, s):
         return ref[pl.ds(16 * s, 16)].reshape(256, 256)
 
+    arrive("q3")
+    c3[y, c, x] = z3[x]
+    quarter("c3", c3)
     arrive("q1")
     scatter("c1", c1)
     twin("c0", "t0", c0)
     arrive("q2")
-    c2[y, c, x] = z2[x]
-    quarter("c2", c2)
-    arrive("q3")
-    c3[y, c, x] = z3[x]
-    quarter("c3", c3)
+    c2[y, c] = z2[...]
+    scatter("c2", c2)
     arrive("msg")
     flipped = jnp.transpose(m0[...].reshape(256, 128).astype(f32))
     rs_[...] = flipped
@@ -279,7 +279,6 @@
     planes("c4", "x4", c4)
 
     twin("c1", "t1", c1)
-    planes("c2", "x2", c2)
     arrive("q0")
     scatter("c5", c5)
     arrive("t1")
@@ -297,13 +296,13 @@
     u = -mm(own, blocks(n5, zp))
     for s in range(2):
         u = u + mm(hh[pair + s, 2], blocks(b5, s))
+    planes("c3", "x3", c3)
     arrive("u4")
     u = u - mm(u4g[1 - zp], blocks(n5, 1 - zp))
     own = u.astype(bf16)
     u5g[zq] = own
     along("u5", 4, u5g, zq)
 
-    planes("c3", "x3", c3)
     arrive("zx")
     loads[6].wait()
     zr4 = zxr[:, 0].reshape(64, 128)
@@ -317,8 +316,7 @@
     lws[:, 1] = imag.astype(bf16)
     for k in range(1, 4):
         send("lw", lws.at[flip(x, k)], lwr.at[k - 1], dev(z, y, c, flip(x, k)))
-    twin("x2", "t2", c2)
-    twin("x4", "t4", c4)
+    twin("c2", "t2", c2)
     arrive("t2")
     for s in range(4):
         b6[16 * s : 16 * s + 16] = square(c2[:, :, s]).reshape(16, 16, 256)
@@ -334,19 +332,8 @@
     own = u.astype(bf16)
     u6g[z] = own
     along("u6", 8, u6g, z)
-
-    twin("x3", "t3", c3)
-    arrive("t3")
-    for s in range(8):
-        b7[16 * s : 16 * s + 16] = square(c3[:, :, s // 2, s % 2]).reshape(16, 16, 256)
-    lax.fori_loop(0, 128, move(6, 0, b7, n7), 0, unroll=8)
-    for k in range(3, 7):
-        got["h"][k].wait_recv()
-    u = -mm(own, blocks(n7, z))
-    for s in range(8):
-        u = u + mm(hh[s, 0], blocks(b7, s))
-
-    twin("c5", "t5", c5)
+    twin("x4", "t4", c4)
+
     arrive("t4")
     v5 = rs_[64:80]
     for s in range(2):
@@ -380,6 +367,18 @@
         for t in range(1, 4):
             total = total + mm(w6[t], route(5, quad + s, t))
         wq6[s] = total * sign_lane
+
+    twin("x3", "t3", c3)
+    twin("c5", "t5", c5)
+    arrive("t3")
+    for s in range(8):
+        b7[16 * s : 16 * s + 16] = square(c3[:, :, s // 2, s % 2]).reshape(16, 16, 256)
+    lax.fori_loop(0, 128, move(6, 0, b7, n7), 0, unroll=8)
+    for k in range(3, 7):
+        got["h"][k].wait_recv()
+    u = -mm(own, blocks(n7, z))
+    for s in range(8):
+        u = u + mm(hh[s, 0], blocks(b7, s))
 
     for k in (1, 7, 2, 6, 3, 5, 4):
         by["u6", k - 1].wait_recv()

time: 51.6 us -> 48.3 us (0.936)
  Pallas kernels: 48.9 us -> 45.6 us
    pallas_call x1, Pallas kernels: 48.9 us -> 45.6 us  [body(): pl.pallas_call(kernel, out_shape=(jax.ShapeDtypeStruct((2, 16, 512), f32)...]
where the time goes in v6:
time: 48.3 us; the launch traced here: 48.2 us
  Pallas kernels  45.6 us (94%)
  between operations  1.29 us (3%)
  local copies, waits for them, and re-layouts  1.25 us (3%)
    pallas_call x1, Pallas kernels, body(): pl.pallas_call(kernel, out_shape=(jax.ShapeDtypeStruct((2, 16, 512), f32)...  45.6 us
    unnamed x2, local copies, waits for them, and re-layouts  1.25 us

profile of v6, /device:TPU:1, one launch (start us, length us, event | category | flops | bytes accessed | tf_op | source)
XLA Modules:
  0.0 48.2 jit_solution(2918455346250860871)
XLA Ops:
  1.3 45.6 %shard_map.95 = (f32[2,16,512]{2,1,0:T(8,128)S(1)}, f32[2,7,8,16]{3,2,1,0:T(8,128)S(1)}) custom-call(f32[2,16,512]{2,1,0:T(8,128)} %rhs_hbm.1, f32[2,7,8,16]{3,2,1,0:T(8,128)} %bitcast.4, bf16[2,128,512]{2,1,0:T(8,128)(2,1)} %inv_hbm.1, bf16[2,8,512]{2,1,0:T(8,128)(2,1)} %bitcast.5, bf16[2,8,2032]{2,1,0:T(8,128)(2,1)} %sinv_hbm.1, ...), custom_call_target="tpu_custom_call" | custom-call | tf_op jit(solution)/shard_map/pallas_call | solution.py:487
  46.9 0.6 %copy.13 = f32[2,16,512]{2,1,0:T(8,128)} copy(f32[2,16,512]{2,1,0:T(8,128)S(1)} %get-tuple-element.8) | data formatting | bytes 131072
  47.5 0.6 %copy.14 = f32[2,16,7,8]{1,3,2,0:T(8,128)} copy(f32[2,16,7,8]{1,3,2,0:T(8,128)S(1)} %bitcast.3) | data formatting | bytes 14336

commit v7 on v6

--- a/solution.py
+++ b/solution.py
@@ -190,9 +190,9 @@
 
     for k in far:
         send("q3", p3.at[flip(z, k)], z3.at[lax.div(z, 2), zp], dev(flip(z, k), y, c, x), k - 1)
-    scatter("c0", c0)
     for ky, kc in layer:
         send("msg", m0.at[y, c], m0.at[y, c], dev(z, flip(y, ky), flip(c, kc), x))
+    scatter("c0", c0)
     send("q1", p1.at[1 - zp], c1.at[y, c, zp], dev(flip(z, 1), y, c, x))
     for k in range(1, 4):
         send("q2", p2.at[flip(zq, k)], z2.at[zq], dev(flip(z, k), y, c, x))

time: 48.3 us -> 50 us (1.035)
  Pallas kernels: 45.6 us -> 47.4 us
    pallas_call x1, Pallas kernels: 45.6 us -> 47.4 us  [body(): pl.pallas_call(kernel, out_shape=(jax.ShapeDtypeStruct((2, 16, 512), f32)...]
where the time goes in v7:
time: 50 us; the launch traced here: 49.9 us
  Pallas kernels  47.4 us (95%)
  between operations  1.29 us (3%)
  local copies, waits for them, and re-layouts  1.25 us (2%)
    pallas_call x1, Pallas kernels, body(): pl.pallas_call(kernel, out_shape=(jax.ShapeDtypeStruct((2, 16, 512), f32)...  47.4 us
    unnamed x2, local copies, waits for them, and re-layouts  1.25 us

profile of v7, /device:TPU:1, one launch (start us, length us, event | category | flops | bytes accessed | tf_op | source)
XLA Modules:
  0.0 49.9 jit_solution(3216962004202891619)
XLA Ops:
  1.3 47.4 %shard_map.95 = (f32[2,16,512]{2,1,0:T(8,128)S(1)}, f32[2,7,8,16]{3,2,1,0:T(8,128)S(1)}) custom-call(f32[2,16,512]{2,1,0:T(8,128)} %rhs_hbm.1, f32[2,7,8,16]{3,2,1,0:T(8,128)} %bitcast.4, bf16[2,128,512]{2,1,0:T(8,128)(2,1)} %inv_hbm.1, bf16[2,8,512]{2,1,0:T(8,128)(2,1)} %bitcast.5, bf16[2,8,2032]{2,1,0:T(8,128)(2,1)} %sinv_hbm.1, ...), custom_call_target="tpu_custom_call" | custom-call | tf_op jit(solution)/shard_map/pallas_call | solution.py:487
  48.6 0.6 %copy.13 = f32[2,16,512]{2,1,0:T(8,128)} copy(f32[2,16,512]{2,1,0:T(8,128)S(1)} %get-tuple-element.8) | data formatting | bytes 131072
  49.3 0.6 %copy.14 = f32[2,16,7,8]{1,3,2,0:T(8,128)} copy(f32[2,16,7,8]{1,3,2,0:T(8,128)S(1)} %bitcast.3) | data formatting | bytes 14336
